TPU v7x, 32 devices: a whole 2x2x4 slice. The times are simulated.
32 devices in a mesh: grp: 2 (over x), ma: 16 (over z, y, core).
Axes of the slice: x: 2, y: 2, z: 4, core: 2. Of those that a mesh axis runs over, the one named last changes fastest.
Arguments:
- vis: float32 [16384, 2, 256], P(('grp', 'ma')), parts along dimension 0, may hold values from -6 to 6
- transfer: bfloat16 [32, 2, 256, 1024], P(('grp', 'ma')), parts along dimension 0, may hold values from -0.1875 to 0.1875
- band_start: int32 [2], P('grp'), parts along dimension 0, may hold values from 0 to 8176
- comp_index: int32 [2048], P(('grp', 'ma')), parts along dimension 0, may hold values from 0 to 16383
- comp_amp: int32 [2048, 2], P(('grp', 'ma')), parts along dimension 0, may hold values from -4096 to 4096
Outputs:
- residual_alm: float32 [32, 2, 1024], P(('grp', 'ma')), parts along dimension 0
There are 2 independent parts, one for each index of `grp`. A program takes and returns all parts, laid end to end along the dimension named above; each array names one. Nothing has to cross between parts.
All inputs are finite; a program needn't handle non-finite values.
Results may differ from a plain program's by a relative error of at most 0.003.
Values sent between devices are 32-bit elements; how exact they have to be, the bound alone decides.
No kernel may reach another device: no remote copies, remote signals or barrier semaphores. Data moves between devices by JAX's collectives and lax.ppermute only.
A program may use at most 64 MiB of HBM per device.

v0:
```python
import math

import jax
import jax.numpy as jnp
from jax import lax
from jax.sharding import PartitionSpec as P

SIDEREAL_TICKS = 8192


def trig_pair_lookup(azimuthal_orders, tick_moments):
    rotation_radians = azimuthal_orders[:, None] * tick_moments[None, :] % SIDEREAL_TICKS
    angle = rotation_radians.astype(jnp.float32) * (2.0 * math.pi / SIDEREAL_TICKS)
    return jnp.concatenate([jnp.cos(angle), jnp.sin(angle)], 0)


def combine_parts(product, row_count):
    product = product.reshape(2, row_count, 2, -1)
    scale = 1.0 / math.sqrt(SIDEREAL_TICKS)
    real_part = (product[0, :, 0] + product[1, :, 1]) * scale
    imag_part = (product[0, :, 1] - product[1, :, 0]) * scale
    return jnp.stack([real_part, imag_part], 1)


def body(vis, transfer, band_start, comp_index, comp_amp):
    ma_count = lax.axis_size("ma")
    device_rank = lax.axis_index("ma")
    m_local = transfer.shape[0]
    width = transfer.shape[3]
    modes = m_local * ma_count
    regrouped = lax.all_to_all(vis, "ma", split_axis=2, concat_axis=0, tiled=True)
    azimuthal_orders = band_start[0] + jnp.arange(modes, dtype=jnp.int32)
    trig_pair = trig_pair_lookup(azimuthal_orders, jnp.arange(SIDEREAL_TICKS, dtype=jnp.int32))
    flat_visibility = regrouped.reshape(SIDEREAL_TICKS, -1)
    product = jnp.dot(
        trig_pair,
        flat_visibility,
        precision=lax.Precision.HIGHEST,
        preferred_element_type=jnp.float32,
    )
    local_spectra = combine_parts(product, modes)
    spectra = lax.all_to_all(local_spectra, "ma", split_axis=0, concat_axis=2, tiled=True)
    index_all, amp_all = (
        lax.all_gather(comp_index, "ma", axis=0, tiled=True),
        lax.all_gather(comp_amp, "ma", axis=0, tiled=True),
    )
    slots = m_local * width
    offset = index_all - device_rank * slots
    inside = (offset >= 0) & (offset < slots)
    target = jnp.where(inside, offset, slots)
    summed = jax.ops.segment_sum(amp_all, target, num_segments=slots + 1)[:slots]
    model_alm = (
        (summed.astype(jnp.float32) * (1.0 / 1024.0))
        .astype(jnp.bfloat16)
        .reshape(m_local, width, 2)
    )
    predicted = jnp.einsum(
        "mcbl,mlk->mcbk", transfer, model_alm, preferred_element_type=jnp.float32
    )
    pred_real = predicted[:, 0, :, 0] - predicted[:, 1, :, 1]
    pred_imag = predicted[:, 0, :, 1] + predicted[:, 1, :, 0]
    resid_vis = (spectra - jnp.stack([pred_real, pred_imag], 1)).astype(jnp.bfloat16)
    projected = jnp.einsum(
        "mcbl,mkb->mkcl", transfer, resid_vis, preferred_element_type=jnp.float32
    )
    alm_real = projected[:, 0, 0] + projected[:, 1, 1]
    alm_imag = projected[:, 1, 0] - projected[:, 0, 1]
    return jnp.stack([alm_real, alm_imag], 1)


def solution(mesh):
    in_specs = (
        P(("grp", "ma"), None, None),
        P(("grp", "ma"), None, None, None),
        P("grp"),
        P(("grp", "ma")),
        P(("grp", "ma"), None),
    )
    out_specs = P(("grp", "ma"), None, None)
    return jax.shard_map(body, mesh=mesh, in_specs=in_specs, out_specs=out_specs, check_vma=False)
```

profile of v0, /device:TPU:0, one launch (start us, length us, event | category | flops | bytes accessed | tf_op | source)
XLA Modules:
  0.0 85.8 jit_solution(13697554280180083877)
XLA Ops:
  0.0 0.0 copy-start
  0.0 3.7 %copy.34 = f32[512,2,256]{0,1,2:T(2,128)} copy(f32[512,2,256]{2,1,0:T(2,128)} %param.5) | data formatting | bytes 2097152 | tf_op args[0]
  3.7 7.4 %all-to-all-start = ((f32[512,2,256]{0,1,2:T(2,128)}), f32[512,2,256]{0,1,2:T(2,128)S(1)}, u32[]{:S(2)}, u32[]{:S(2)}) async-start(f32[512,2,256]{0,1,2:T(2,128)} %copy.34), calls=%async_computation | async-start | bytes 2097152 | tf_op jit(solution)/shard_map/all_to_all | solution.py:31
  11.8 0.0 copy-start.3
  11.8 0.6 copy-done.3
  12.5 0.6 dynamic-slice
  13.7 0.0 copy-start.2
  13.7 0.6 copy-done.2
  14.4 0.2 dynamic-update-slice
  14.5 23.3 %all-reduce = s32[1024]{0:T(1024)S(1)} all-reduce(s32[1024]{0:T(1024)S(1)} %dynamic-update-slice), channel_id=1, replica_groups=mesh['grp'=2,'ma'=16] {'ma'}, use_global_device_ids=true, to_apply=%add | all-reduce | flops 1024 | bytes 8192
  37.8 0.7 copy-done.1
  38.5 19.5 %all-gather = s32[16,64,2]{1,2,0:T(2,128)S(1)} all-gather(s32[1,64,2]{1,2,0:T(2,128)S(1)} %bitcast.60), channel_id=1, replica_groups=mesh['grp'=2,'ma'=16] {'ma'}, dimensions={0}, use_global_device_ids=true | all-gather | bytes 8704 | tf_op jit(solution)/shard_map/all_gather | solution.py:45
  58.0 0.2 copy.43
  58.2 7.3 %scatter_custom_fusion = s32[1025,2]{1,0:T(8,128)S(1)} fusion(s32[1024]{0:T(1024)S(1)} %and_select_fusion, s32[1024,2]{1,0:T(8,128)S(1)} %bitcast.59, s32[]{:T(128)} %constant.9.clone.1), kind=kCustom, calls=%fused_computation.16 | custom fusion | flops 2048 | bytes 8204 | tf_op jit(solution)/shard_map/scatter-add | solution.py:51
  65.6 0.1 multiply_convert_fusion
  65.6 0.1 copy.47
  65.8 0.4 convolution_bitcast_fusion.1
  66.1 2.1 %fusion.11 = (f32[16,8192]{1,0:T(8,128)S(1)}, f32[16,8192]{1,0:T(8,128)S(1)}) fusion(s32[16]{0:T(128)S(1)} %iota_add_fusion), kind=kLoop, calls=%fused_computation.19 | loop fusion | flops 1835008 | bytes 1048640 | tf_op jit(solution)/shard_map/cos | solution.py:14
  68.3 0.1 pad_maximum_fusion
  68.4 0.0 all-to-all-done
  68.4 0.2 copy.35
  68.6 0.6 copy.36
  69.2 0.6 copy.46
  69.8 4.4 %fusion.22 = f32[2,16,2,16]{3,1,2,0:T(8,128)S(1)} fusion(f32[2,16,8192,1]{2,1,3,0:T(8,128)S(1)} %bitcast.55, f32[2,16,8192,1]{2,1,0,3:T(8,128)S(1)} %bitcast.56), kind=kOutput, calls=%fused_computation.41 | convolution fusion | flops 100663296 | bytes 2101248 | tf_op jit(solution)/shard_map/dot_general | solution.py:35
  74.3 0.6 copy.37
  74.9 3.5 %all-to-all-start.1 = ((f32[16,2,16]{2,1,0:T(2,128)}), f32[16,2,16]{2,1,0:T(2,128)S(1)}, u32[]{:S(2)}, u32[]{:S(2)}) async-start(f32[16,2,16]{2,1,0:T(2,128)} %copy.37), calls=%async_computation.1 | async-start | bytes 32768 | tf_op jit(solution)/shard_map/all_to_all | solution.py:42
  78.4 0.1 add.66
  78.5 0.1 sub.60
  78.5 6.3 %all-to-all-done.1 = f32[16,2,16]{2,1,0:T(2,128)S(1)} async-done(((f32[16,2,16]{2,1,0:T(2,128)}), f32[16,2,16]{2,1,0:T(2,128)S(1)}, u32[]{:S(2)}, u32[]{:S(2)}) %all-to-all-start.1) | async-done | bytes 2080 | tf_op jit(solution)/shard_map/all_to_all | solution.py:42
  84.8 0.1 reshape.206
  84.9 0.2 convolution_bitcast_fusion
  85.2 0.6 pad_maximum_fusion.2
  (10 shorter events, 0.1 us)
Async XLA Ops:
  0.0 65.8 %copy-start = (bf16[1,2,256,1024]{3,2,1,0:T(8,128)(2,1)S(1)}, bf16[1,2,256,1024]{3,2,1,0:T(8,128)(2,1)}, u32[]{:S(2)}) copy-start(bf16[1,2,256,1024]{3,2,1,0:T(8,128)(2,1)} %param.6) | copy-start | bytes 3145732
  3.7 64.6 %all-to-all-start = ((f32[512,2,256]{0,1,2:T(2,128)}), f32[512,2,256]{0,1,2:T(2,128)S(1)}, u32[]{:S(2)}, u32[]{:S(2)}) async-start(f32[512,2,256]{0,1,2:T(2,128)} %copy.34), calls=%async_computation | async-start | bytes 2097152 | tf_op jit(solution)/shard_map/all_to_all | solution.py:31
  11.8 0.7 copy-start.3
  13.7 0.7 copy-start.2
  37.8 0.7 copy-start.1
  74.9 9.9 %all-to-all-start.1 = ((f32[16,2,16]{2,1,0:T(2,128)}), f32[16,2,16]{2,1,0:T(2,128)S(1)}, u32[]{:S(2)}, u32[]{:S(2)}) async-start(f32[16,2,16]{2,1,0:T(2,128)} %copy.37), calls=%async_computation.1 | async-start | bytes 32768 | tf_op jit(solution)/shard_map/all_to_all | solution.py:42
where the time goes:
time: 86.1 us; the launch traced here: 85.8 us
  blocking collectives  42.8 us (50%)
  starting transfers between devices  10.9 us (13%)
  other arithmetic  10.2 us (12%)
  local copies, waits for them, and re-layouts  9.1 us (11%)
  waiting for transfers between devices  6.29 us (7%)
  matrix products  5.05 us (6%)
  between operations  1.48 us (2%)
    unnamed x1, blocking collectives  23.3 us
    all_gather x1, blocking collectives, body(): lax.all_gather(comp_amp, 'ma', axis=0, tiled=True)  19.5 us
    unnamed x15, local copies, waits for them, and re-layouts  7.42 us
    all_to_all x1, starting transfers between devices, body(): lax.all_to_all(vis, 'ma', split_axis=2, concat_axis=0, tiled=True)  7.41 us
    scatter-add x1, other arithmetic, body(): jax.ops.segment_sum(amp_all, target, num_segments=slots + 1)[:slots]  7.31 us
    all_to_all x1, waiting for transfers between devices, body(): lax.all_to_all(local_spectra, 'ma', split_axis=0, concat_axis=2, tiled=True)  6.28 us
    dot_general x1, matrix products, body(): jnp.dot(trig_pair, flat_visibility, precision=lax.Precision.HIGHEST, pref...  4.42 us
    all_to_all x1, starting transfers between devices, body(): lax.all_to_all(local_spectra, 'ma', split_axis=0, concat_axis=2, tiled=True)  3.47 us
  transfers between devices with their start and end apart: 2, of which 1 were waited for; matrix products, arithmetic and copies ran while one was open for 13% of the time, Pallas kernels for 0%

commit v1 on v0

v1 whole, which is shorter than its diff:
```python
import functools
import math

import jax
import jax.numpy as jnp
from jax import lax
from jax.experimental import pallas as pl
from jax.experimental.pallas import tpu as pltpu
from jax.sharding import PartitionSpec as P

LANES = 128
SPLIT = 64
UNIT = 1.0 / 1024.0


def padded(count, unit):
    return -(-count // unit) * unit


def cos_sin(phase, ticks):
    quarter = ticks // 4
    quadrant = (phase + quarter // 2) // quarter
    theta = (phase - quadrant * quarter).astype(jnp.float32) * (2.0 * math.pi / ticks)
    sq = theta * theta
    sine = theta * (1.0 + sq * (-1.0 / 6 + sq * (1.0 / 120 + sq * (-1.0 / 5040 + sq * (1.0 / 362880)))))
    cosine = 1.0 + sq * (-0.5 + sq * (1.0 / 24 + sq * (-1.0 / 720 + sq * (1.0 / 40320 - sq * (1.0 / 3628800)))))
    odd = (quadrant & 1) == 1
    cos_value = jnp.where(odd, sine, cosine)
    sin_value = jnp.where(odd, cosine, sine)
    cos_value = jnp.where(((quadrant + 1) & 2) == 2, -cos_value, cos_value)
    sin_value = jnp.where((quadrant & 2) == 2, -sin_value, sin_value)
    return cos_value, sin_value


def halves(value):
    high = value.astype(jnp.bfloat16)
    low = (value - high.astype(jnp.float32)).astype(jnp.bfloat16)
    return high, low


def transform_kernel(ticks, modes, m_local, comps, band_ref, vis_hbm, index_ref, amp_ref, out_ref, vis_ref, sem):
    copy = pltpu.make_async_copy(vis_hbm, vis_ref, sem)
    copy.start()
    rank = lax.axis_index("ma")
    devices = modes // m_local
    samples = ticks // devices
    pieces = vis_ref.shape[0] // samples
    tiles = pieces // 2
    order = band_ref[0] + lax.broadcasted_iota(jnp.int32, (modes, samples), 0)
    moment = rank * samples + lax.broadcasted_iota(jnp.int32, (modes, samples), 1)
    cos_value, sin_value = cos_sin((order * moment) % ticks, ticks)
    cos_high, cos_low = halves(cos_value)
    sin_high, sin_low = halves(sin_value)
    table = jnp.concatenate([cos_high, sin_high, cos_low, sin_low], 0)

    first = m_local * pieces
    chunks = padded(comps, LANES) // LANES
    for chunk in range(chunks):
        size = min(LANES, comps - chunk * LANES)
        for which in range(3):
            source = index_ref[...] if which == 0 else amp_ref[which - 1 : which, :]
            row = source[:, chunk * LANES : chunk * LANES + size].astype(jnp.float32)
            if size < LANES:
                row = jnp.concatenate([row, jnp.zeros((1, LANES - size), jnp.float32)], 1)
            out_ref[:, first + which * chunks + chunk, :] = jnp.broadcast_to(row, (devices, LANES))
    for spare in range(first + 3 * chunks, out_ref.shape[1]):
        out_ref[:, spare, :] = jnp.zeros((devices, LANES), jnp.float32)

    copy.wait()
    scale = 1.0 / math.sqrt(ticks)
    for tile in range(tiles):
        parts = [vis_ref[pl.ds(tile * 2 + part, samples, stride=pieces), :] for part in range(2)]
        high, low = halves(jnp.concatenate(parts, 1))
        product = jnp.dot(table, high, preferred_element_type=jnp.float32)
        product += jnp.dot(table, low, preferred_element_type=jnp.float32)
        product = product[: 2 * modes] + product[2 * modes :]
        from_cos, from_sin = product[:modes], product[modes:]
        real_part = (from_cos[:, :LANES] + from_sin[:, LANES:]) * scale
        imag_part = (from_cos[:, LANES:] - from_sin[:, :LANES]) * scale
        for local in range(m_local):
            rows = (local * pieces + tile, local * pieces + tiles + tile)
            if m_local == 1:
                out_ref[:, rows[0], :] = real_part
                out_ref[:, rows[1], :] = imag_part
            else:
                for device in range(devices):
                    mode = device * m_local + local
                    out_ref[device, rows[0] : rows[0] + 1, :] = real_part[mode : mode + 1]
                    out_ref[device, rows[1] : rows[1] + 1, :] = imag_part[mode : mode + 1]


def residual_kernel(m_local, pieces, chunks, got_ref, transfer_ref, out_ref):
    devices = got_ref.shape[0]
    baselines, width = transfer_ref.shape[2], transfer_ref.shape[3]
    tiles = pieces // 2
    groups = width // LANES
    base = lax.axis_index("ma") * (m_local * width)
    first = m_local * pieces
    spectra = got_ref[0]
    for device in range(1, devices):
        spectra += got_ref[device]

    def rows_of(which, chunk):
        return got_ref[:, first + which * chunks + chunk, :].astype(jnp.int32)

    offsets, amplitudes = [], []
    for chunk in range(chunks):
        offsets.append(rows_of(0, chunk) - base)
        amplitudes.append((rows_of(1, chunk), rows_of(2, chunk)))

    for local in range(m_local):
        selected, places = [], []
        for chunk in range(chunks):
            offset = offsets[chunk] - local * width
            group, place = offset // LANES, offset % LANES
            for device in range(devices):
                here = group[device : device + 1] == lax.broadcasted_iota(jnp.int32, (groups, LANES), 0)
                column = []
                for amplitude in amplitudes[chunk]:
                    value = amplitude[device : device + 1]
                    for part in (value // SPLIT, value % SPLIT):
                        column.append(jnp.where(here, part.astype(jnp.float32), 0.0))
                selected.append(jnp.concatenate(column, 0).astype(jnp.bfloat16))
                match = place[device : device + 1] == lax.broadcasted_iota(jnp.int32, (LANES, LANES), 0)
                places.append(jnp.where(match, 1.0, 0.0).astype(jnp.bfloat16))
        counted = lax.dot_general(
            jnp.concatenate(selected, 1),
            jnp.concatenate(places, 1),
            (((1,), (1,)), ((), ())),
            preferred_element_type=jnp.float32,
        ).astype(jnp.int32)
        model = []
        for part in range(2):
            high = counted[2 * part * groups : (2 * part + 1) * groups]
            low = counted[(2 * part + 1) * groups : (2 * part + 2) * groups]
            alm = (high * SPLIT + low).astype(jnp.float32) * UNIT
            model.append(jnp.concatenate([alm[g : g + 1] for g in range(groups)], 1))
        model_alm = jnp.concatenate(model, 0).astype(jnp.bfloat16)

        real_matrix, imag_matrix = transfer_ref[local, 0], transfer_ref[local, 1]
        contract = (((1,), (1,)), ((), ()))
        by_real = lax.dot_general(model_alm, real_matrix, contract, preferred_element_type=jnp.float32)
        by_imag = lax.dot_general(model_alm, imag_matrix, contract, preferred_element_type=jnp.float32)
        pred_real = by_real[0:1] - by_imag[1:2]
        pred_imag = by_real[1:2] + by_imag[0:1]
        start = local * pieces
        spectrum = [
            jnp.concatenate([spectra[start + part * tiles + t : start + part * tiles + t + 1] for t in range(tiles)], 1)
            for part in range(2)
        ]
        resid_real = (spectrum[0] - pred_real).astype(jnp.bfloat16)
        resid_imag = (spectrum[1] - pred_imag).astype(jnp.bfloat16)
        with_real = jnp.concatenate([resid_real, resid_imag], 0)
        with_imag = jnp.concatenate([resid_imag, -resid_real], 0)
        out_ref[local] = jnp.dot(with_real, real_matrix, preferred_element_type=jnp.float32) + jnp.dot(
            with_imag, imag_matrix, preferred_element_type=jnp.float32
        )


def body(vis, transfer, band_start, comp_index, comp_amp):
    devices = lax.axis_size("ma")
    samples, _, baselines = vis.shape
    m_local, _, _, width = transfer.shape
    comps = comp_index.shape[0]
    tiles = baselines // LANES
    pieces = 2 * tiles
    chunks = padded(comps, LANES) // LANES
    rows = padded(m_local * pieces + 3 * chunks, 8)
    vmem, smem = pl.BlockSpec(memory_space=pltpu.VMEM), pl.BlockSpec(memory_space=pltpu.SMEM)
    lines = vis.reshape(samples, 2, tiles, LANES).transpose(0, 2, 1, 3).reshape(samples * pieces, LANES)
    send = pl.pallas_call(
        functools.partial(transform_kernel, samples * devices, m_local * devices, m_local, comps),
        out_shape=jax.ShapeDtypeStruct((devices, rows, LANES), jnp.float32),
        in_specs=[smem, pl.BlockSpec(memory_space=pl.ANY), vmem, vmem],
        out_specs=vmem,
        scratch_shapes=[pltpu.VMEM((samples * pieces, LANES), jnp.float32), pltpu.SemaphoreType.DMA],
        name="transform",
    )(band_start, lines, comp_index.reshape(1, comps), comp_amp.T)
    got = lax.all_to_all(send, "ma", split_axis=0, concat_axis=0, tiled=True)
    return pl.pallas_call(
        functools.partial(residual_kernel, m_local, pieces, chunks),
        out_shape=jax.ShapeDtypeStruct((m_local, 2, width), jnp.float32),
        in_specs=[vmem, vmem],
        out_specs=vmem,
        name="residual",
    )(got, transfer)


def solution(mesh):
    in_specs = (
        P(("grp", "ma"), None, None),
        P(("grp", "ma"), None, None, None),
        P("grp"),
        P(("grp", "ma")),
        P(("grp", "ma"), None),
    )
    out_specs = P(("grp", "ma"), None, None)
    return jax.shard_map(body, mesh=mesh, in_specs=in_specs, out_specs=out_specs, check_vma=False)
```

time: 86.1 us -> 21.2 us (0.25)
  blocking collectives: 42.8 us -> 14.4 us
  starting transfers between devices: 10.9 us -> 0 us
  other arithmetic: 10.2 us -> 0 us
  local copies, waits for them, and re-layouts: 9.1 us -> 0 us
  waiting for transfers between devices: 6.29 us -> 0 us
  Pallas kernels: 0 us -> 5.87 us
  matrix products: 5.05 us -> 0 us
    unnamed x1 -> x0, blocking collectives: 23.3 us -> none
    all_gather x1 -> x0, blocking collectives: 19.5 us -> none  [body(): lax.all_gather(comp_amp, 'ma', axis=0, tiled=True)]
    all_to_all x0 -> x1, blocking collectives: none -> 14.4 us  [body(): got = lax.all_to_all(send, 'ma', split_axis=0, concat_axis=0, tiled=True)]
    all_to_all x2 -> x0, starting transfers between devices: 10.9 us -> none  [the longest x1 7.41 us: body(): lax.all_to_all(vis, 'ma', split_axis=2, concat_axis=0, tiled=True)]
    unnamed x15 -> x0, local copies, waits for them, and re-layouts: 7.42 us -> none
    scatter-add x1 -> x0, other arithmetic: 7.31 us -> none  [body(): jax.ops.segment_sum(amp_all, target, num_segments=slots + 1)[:slots]]
    all_to_all x2 -> x0, waiting for transfers between devices: 6.29 us -> none  [the longest x1 6.28 us: body(): lax.all_to_all(local_spectra, 'ma', split_axis=0, concat_axis=2, tiled=True)]
    pallas_call x0 -> x2, Pallas kernels: none -> 5.87 us  [the longest x1 2.95 us: body(): pl.pallas_call(functools.partial(residual_kernel, m_local, pieces, chunks...]
  transfers between devices with their start and end apart: 2 -> 0, of which waited for: 1 -> 0; matrix products, arithmetic and copies ran while one was open for 13% -> 0% of each run, Pallas kernels for 0% -> 0%
where the time goes in v1:
time: 21.2 us; the launch traced here: 21 us
  blocking collectives  14.4 us (68%)
  Pallas kernels  5.87 us (28%)
  between operations  0.66 us (3%)
    all_to_all x1, blocking collectives, body(): got = lax.all_to_all(send, 'ma', split_axis=0, concat_axis=0, tiled=True)  14.4 us
    pallas_call x1, Pallas kernels, body(): pl.pallas_call(functools.partial(residual_kernel, m_local, pieces, chunks...  2.95 us
    pallas_call x1, Pallas kernels, body(): pl.pallas_call(functools.partial(transform_kernel, samples * devices, m_l...  2.91 us

profile of v1, /device:TPU:0, one launch (start us, length us, event | category | flops | bytes accessed | tf_op | source)
XLA Modules:
  0.0 21.0 jit_solution(31128631807819250)
XLA Ops:
  0.7 2.9 %transform.1 = f32[16,8,128]{2,1,0:T(8,128)} custom-call(s32[1]{0:T(128)S(6)} %copy.7.band_ref, f32[2048,128]{1,0:T(8,128)} %bitcast.7, s32[1,64]{1,0:T(1,128)} %bitcast.9, s32[2,64]{1,0:T(2,128)} %bitcast.8), custom_call_target="tpu_custom_call" | custom-call | tf_op jit(solution)/shard_map/transform/pallas_call | solution.py:171
  3.6 14.4 %all_to_all.5.got_ref = f32[16,8,128]{2,1,0:T(8,128)} all-to-all(f32[16,8,128]{2,1,0:T(8,128)} %transform.1), channel_id=1, replica_groups=mesh['grp'=2,'ma'=16] {'ma'}, dimensions={0} | all-to-all | bytes 131072 | tf_op jit(solution)/shard_map/all_to_all | solution.py:179
  18.0 3.0 %residual.1 = f32[1,2,1024]{2,1,0:T(2,128)} custom-call(f32[16,8,128]{2,1,0:T(8,128)} %all_to_all.5.got_ref, bf16[1,2,256,1024]{3,2,1,0:T(8,128)(2,1)} %transfer_ref.1), custom_call_target="tpu_custom_call" | custom-call | tf_op jit(solution)/shard_map/residual/pallas_call | solution.py:180

commit v2 on v1

--- a/solution.py
+++ b/solution.py
@@ -11,6 +11,7 @@
 LANES = 128
 SPLIT = 64
 UNIT = 1.0 / 1024.0
+VMEM_LIMIT = 32 * 2**20
 
 
 def padded(count, unit):
@@ -38,9 +39,17 @@
     return high, low
 
 
-def transform_kernel(ticks, modes, m_local, comps, band_ref, vis_hbm, index_ref, amp_ref, out_ref, vis_ref, sem):
-    copy = pltpu.make_async_copy(vis_hbm, vis_ref, sem)
-    copy.start()
+def transform_kernel(ticks, modes, m_local, comps, *refs):
+    band_ref, vis_hbm, index_hbm, amp_hbm, transfer_hbm, out_ref, transfer_ref, index_ref, amp_ref, vis_ref, sems = refs
+    vis_copy = pltpu.make_async_copy(vis_hbm, vis_ref, sems.at[3])
+    vis_copy.start()
+    copies = [
+        pltpu.make_async_copy(index_hbm, index_ref, sems.at[0]),
+        pltpu.make_async_copy(amp_hbm, amp_ref, sems.at[1]),
+        pltpu.make_async_copy(transfer_hbm, transfer_ref, sems.at[2]),
+    ]
+    for copy in copies:
+        copy.start()
     rank = lax.axis_index("ma")
     devices = modes // m_local
     samples = ticks // devices
@@ -53,20 +62,7 @@
     sin_high, sin_low = halves(sin_value)
     table = jnp.concatenate([cos_high, sin_high, cos_low, sin_low], 0)
 
-    first = m_local * pieces
-    chunks = padded(comps, LANES) // LANES
-    for chunk in range(chunks):
-        size = min(LANES, comps - chunk * LANES)
-        for which in range(3):
-            source = index_ref[...] if which == 0 else amp_ref[which - 1 : which, :]
-            row = source[:, chunk * LANES : chunk * LANES + size].astype(jnp.float32)
-            if size < LANES:
-                row = jnp.concatenate([row, jnp.zeros((1, LANES - size), jnp.float32)], 1)
-            out_ref[:, first + which * chunks + chunk, :] = jnp.broadcast_to(row, (devices, LANES))
-    for spare in range(first + 3 * chunks, out_ref.shape[1]):
-        out_ref[:, spare, :] = jnp.zeros((devices, LANES), jnp.float32)
-
-    copy.wait()
+    vis_copy.wait()
     scale = 1.0 / math.sqrt(ticks)
     for tile in range(tiles):
         parts = [vis_ref[pl.ds(tile * 2 + part, samples, stride=pieces), :] for part in range(2)]
@@ -87,6 +83,22 @@
                     mode = device * m_local + local
                     out_ref[device, rows[0] : rows[0] + 1, :] = real_part[mode : mode + 1]
                     out_ref[device, rows[1] : rows[1] + 1, :] = imag_part[mode : mode + 1]
+
+    first = m_local * pieces
+    chunks = padded(comps, LANES) // LANES
+    copies[0].wait()
+    copies[1].wait()
+    for chunk in range(chunks):
+        size = min(LANES, comps - chunk * LANES)
+        for which in range(3):
+            source = index_ref[...] if which == 0 else amp_ref[which - 1 : which, :]
+            row = source[:, chunk * LANES : chunk * LANES + size].astype(jnp.float32)
+            if size < LANES:
+                row = jnp.concatenate([row, jnp.zeros((1, LANES - size), jnp.float32)], 1)
+            out_ref[:, first + which * chunks + chunk, :] = jnp.broadcast_to(row, (devices, LANES))
+    for spare in range(first + 3 * chunks, out_ref.shape[1]):
+        out_ref[:, spare, :] = jnp.zeros((devices, LANES), jnp.float32)
+    copies[2].wait()
 
 
 def residual_kernel(m_local, pieces, chunks, got_ref, transfer_ref, out_ref):
@@ -157,6 +169,14 @@
         )
 
 
+def in_hbm(value):
+    return pltpu.with_memory_space_constraint(value, pltpu.HBM)
+
+
+def in_vmem(value):
+    return pltpu.with_memory_space_constraint(value, pltpu.VMEM)
+
+
 def body(vis, transfer, band_start, comp_index, comp_amp):
     devices = lax.axis_size("ma")
     samples, _, baselines = vis.shape
@@ -166,24 +186,31 @@
     pieces = 2 * tiles
     chunks = padded(comps, LANES) // LANES
     rows = padded(m_local * pieces + 3 * chunks, 8)
-    vmem, smem = pl.BlockSpec(memory_space=pltpu.VMEM), pl.BlockSpec(memory_space=pltpu.SMEM)
+    vmem, smem, hbm = (pl.BlockSpec(memory_space=space) for space in (pltpu.VMEM, pltpu.SMEM, pltpu.HBM))
     lines = vis.reshape(samples, 2, tiles, LANES).transpose(0, 2, 1, 3).reshape(samples * pieces, LANES)
-    send = pl.pallas_call(
+    send, matrices = pl.pallas_call(
         functools.partial(transform_kernel, samples * devices, m_local * devices, m_local, comps),
-        out_shape=jax.ShapeDtypeStruct((devices, rows, LANES), jnp.float32),
-        in_specs=[smem, pl.BlockSpec(memory_space=pl.ANY), vmem, vmem],
-        out_specs=vmem,
-        scratch_shapes=[pltpu.VMEM((samples * pieces, LANES), jnp.float32), pltpu.SemaphoreType.DMA],
+        out_shape=(pltpu.VMEM((devices, rows, LANES), jnp.float32), pltpu.VMEM(transfer.shape, transfer.dtype)),
+        in_specs=[smem, hbm, hbm, hbm, hbm],
+        out_specs=(vmem, vmem),
+        scratch_shapes=[
+            pltpu.VMEM((1, comps), jnp.int32),
+            pltpu.VMEM((2, comps), jnp.int32),
+            pltpu.VMEM(lines.shape, lines.dtype),
+            pltpu.SemaphoreType.DMA((4,)),
+        ],
+        compiler_params=pltpu.CompilerParams(vmem_limit_bytes=VMEM_LIMIT),
         name="transform",
-    )(band_start, lines, comp_index.reshape(1, comps), comp_amp.T)
+    )(band_start, in_hbm(lines), in_hbm(comp_index.reshape(1, comps)), in_hbm(comp_amp.T), in_hbm(transfer))
     got = lax.all_to_all(send, "ma", split_axis=0, concat_axis=0, tiled=True)
     return pl.pallas_call(
         functools.partial(residual_kernel, m_local, pieces, chunks),
         out_shape=jax.ShapeDtypeStruct((m_local, 2, width), jnp.float32),
         in_specs=[vmem, vmem],
         out_specs=vmem,
+        compiler_params=pltpu.CompilerParams(vmem_limit_bytes=VMEM_LIMIT),
         name="residual",
-    )(got, transfer)
+    )(in_vmem(got), in_vmem(matrices))
 
 
 def solution(mesh):

time: 21.2 us -> 18.3 us (0.86)
  Pallas kernels: 5.87 us -> 3.34 us
  blocking collectives: 14.4 us -> 14.1 us
    pallas_call x1, Pallas kernels: 2.95 us -> 1.69 us  [body(): pl.pallas_call(functools.partial(residual_kernel, m_local, pieces, chunks...]
    pallas_call x1, Pallas kernels: 2.91 us -> 1.65 us  [body(): pl.pallas_call(functools.partial(transform_kernel, samples * devices, m_l...]
    all_to_all x1, blocking collectives: 14.4 us -> 14.1 us  [body(): got = lax.all_to_all(send, 'ma', split_axis=0, concat_axis=0, tiled=True)]
where the time goes in v2:
time: 18.3 us; the launch traced here: 18.1 us
  blocking collectives  14.1 us (77%)
  Pallas kernels  3.34 us (18%)
  between operations  0.66 us (4%)
    all_to_all x1, blocking collectives, body(): got = lax.all_to_all(send, 'ma', split_axis=0, concat_axis=0, tiled=True)  14.1 us
    pallas_call x1, Pallas kernels, body(): pl.pallas_call(functools.partial(residual_kernel, m_local, pieces, chunks...  1.69 us
    pallas_call x1, Pallas kernels, body(): pl.pallas_call(functools.partial(transform_kernel, samples * devices, m_l...  1.65 us

profile of v2, /device:TPU:0, one launch (start us, length us, event | category | flops | bytes accessed | tf_op | source)
XLA Modules:
  0.0 18.1 jit_solution(11469727908881625010)
XLA Ops:
  0.7 1.7 %transform.1 = (f32[16,8,128]{2,1,0:T(8,128)S(1)}, bf16[1,2,256,1024]{3,2,1,0:T(8,128)(2,1)S(1)}) custom-call(s32[1]{0:T(128)S(6)} %copy.7.refs_0_, f32[2048,128]{1,0:T(8,128)} %bitcast.7, s32[1,64]{1,0:T(1,128)} %bitcast.9, s32[2,64]{1,0:T(2,128)} %bitcast.8, bf16[1,2,256,1024]{3,2,1,0:T(8,128)(2,1)} %refs_4_.1), custom_call_target="tpu_custom_call" | custom-call | tf_op jit(solution)/shard_map/transform/pallas_call | solution.py:191
  2.3 14.1 %all_to_all.5.got_ref = f32[16,8,128]{2,1,0:T(8,128)S(1)} all-to-all(f32[16,8,128]{2,1,0:T(8,128)S(1)} %get-tuple-element.7), channel_id=1, replica_groups=mesh['grp'=2,'ma'=16] {'ma'}, dimensions={0} | all-to-all | bytes 131072 | tf_op jit(solution)/shard_map/all_to_all | solution.py:205
  16.4 1.7 %residual.1 = f32[1,2,1024]{2,1,0:T(2,128)} custom-call(f32[16,8,128]{2,1,0:T(8,128)S(1)} %all_to_all.5.got_ref, bf16[1,2,256,1024]{3,2,1,0:T(8,128)(2,1)S(1)} %get-tuple-element.8.transfer_ref), custom_call_target="tpu_custom_call" | custom-call | tf_op jit(solution)/shard_map/residual/pallas_call | solution.py:206

commit v3 on v2

v3 whole, which is shorter than its diff:
```python
import functools
import math

import jax
import jax.numpy as jnp
from jax import lax
from jax.experimental import pallas as pl
from jax.experimental.pallas import tpu as pltpu
from jax.sharding import PartitionSpec as P

LANES = 128
SPLIT = 64
UNIT = 1.0 / 1024.0
VMEM_LIMIT = 32 * 2**20


def padded(count, unit):
    return -(-count // unit) * unit


def cos_sin(phase, ticks):
    quarter = ticks // 4
    quadrant = (phase + quarter // 2) // quarter
    theta = (phase - quadrant * quarter).astype(jnp.float32) * (2.0 * math.pi / ticks)
    sq = theta * theta
    sine = theta * (1.0 + sq * (-1.0 / 6 + sq * (1.0 / 120 + sq * (-1.0 / 5040 + sq * (1.0 / 362880)))))
    cosine = 1.0 + sq * (-0.5 + sq * (1.0 / 24 + sq * (-1.0 / 720 + sq * (1.0 / 40320 - sq * (1.0 / 3628800)))))
    odd = (quadrant & 1) == 1
    cos_value = jnp.where(odd, sine, cosine)
    sin_value = jnp.where(odd, cosine, sine)
    cos_value = jnp.where(((quadrant + 1) & 2) == 2, -cos_value, cos_value)
    sin_value = jnp.where((quadrant & 2) == 2, -sin_value, sin_value)
    return cos_value, sin_value


def halves(value):
    high = value.astype(jnp.bfloat16)
    low = (value - high.astype(jnp.float32)).astype(jnp.bfloat16)
    return high, low


def offsets_of(devices):
    return [1] + [step | 1 for step in (1 << bit for bit in range(1, devices.bit_length() - 1))]


def slot_size(comps):
    if comps >= LANES:
        return padded(comps, LANES)
    return 1 << (comps - 1).bit_length()


def transform_kernel(ticks, modes, m_local, comps, *refs):
    band_ref, vis_hbm, index_hbm, amp_hbm, transfer_hbm = refs[:5]
    send_ref, keep_ref, transfer_ref, index_ref, amp_ref, vis_ref, sems = refs[5:]
    vis_copy = pltpu.make_async_copy(vis_hbm, vis_ref, sems.at[3])
    vis_copy.start()
    copies = [
        pltpu.make_async_copy(index_hbm, index_ref, sems.at[0]),
        pltpu.make_async_copy(amp_hbm, amp_ref, sems.at[1]),
        pltpu.make_async_copy(transfer_hbm, transfer_ref, sems.at[2]),
    ]
    for copy in copies:
        copy.start()
    rank = lax.axis_index("ma")
    devices = modes // m_local
    samples = ticks // devices
    pieces = vis_ref.shape[0] // samples
    tiles = pieces // 2
    row = lax.broadcasted_iota(jnp.int32, (modes, samples), 0)
    position = row % devices
    receiver = jnp.broadcast_to(rank, (modes, samples))
    for step, offset in enumerate(offsets_of(devices)):
        receiver ^= jnp.where((position & (devices >> (step + 1))) == 0, offset, 0)
    order = band_ref[0] + receiver * m_local + row // devices
    moment = rank * samples + lax.broadcasted_iota(jnp.int32, (modes, samples), 1)
    cos_value, sin_value = cos_sin((order * moment) % ticks, ticks)
    cos_high, cos_low = halves(cos_value)
    sin_high, sin_low = halves(sin_value)
    table = jnp.concatenate([cos_high, sin_high, cos_low, sin_low], 0)

    half, size = devices // 2, m_local * pieces
    first = send_ref.shape[0] - half * size
    vis_copy.wait()
    scale = 1.0 / math.sqrt(ticks)
    for tile in range(tiles):
        parts = [vis_ref[pl.ds(tile * 2 + part, samples, stride=pieces), :] for part in range(2)]
        high, low = halves(jnp.concatenate(parts, 1))
        product = jnp.dot(table, high, preferred_element_type=jnp.float32)
        product += jnp.dot(table, low, preferred_element_type=jnp.float32)
        product = product[: 2 * modes] + product[2 * modes :]
        from_cos, from_sin = product[:modes], product[modes:]
        real_part = (from_cos[:, :LANES] + from_sin[:, LANES:]) * scale
        imag_part = (from_cos[:, LANES:] - from_sin[:, :LANES]) * scale
        for local in range(m_local):
            for part, value in enumerate((real_part, imag_part)):
                start = first + local * pieces + part * tiles + tile
                at = local * devices
                send_ref[pl.ds(start, half, stride=size), :] = value[at : at + half]
                keep_ref[pl.ds(start, half, stride=size), :] = value[at + half : at + devices]

    slot = slot_size(comps)
    lines = max(1, slot // LANES)
    width = slot // lines
    send_ref[:first] = jnp.zeros((first, LANES), jnp.float32)
    keep_ref[:first] = jnp.zeros((first, LANES), jnp.float32)
    copies[0].wait()
    copies[1].wait()
    lane = lax.broadcasted_iota(jnp.int32, (1, LANES), 1)
    mine = lane // width == rank % (LANES // width)
    for which in range(3):
        source = index_ref[...] if which == 0 else amp_ref[which - 1 : which, :]
        for line in range(lines):
            value = source[:, line * width : (line + 1) * width].astype(jnp.float32)
            if value.shape[1] < width:
                value = jnp.concatenate([value, jnp.zeros((1, width - value.shape[1]), jnp.float32)], 1)
            value = jnp.where(mine, jnp.concatenate([value] * (LANES // width), 1), 0.0)
            at = which * (first // 3) + rank * slot // LANES + line
            send_ref[pl.ds(at, 1), :] = value
            keep_ref[pl.ds(at, 1), :] = value
    copies[2].wait()


def residual_kernel(m_local, pieces, held_ref, got_ref, transfer_ref, out_ref):
    width = transfer_ref.shape[3]
    tiles = pieces // 2
    groups = width // LANES
    base = lax.axis_index("ma") * (m_local * width)
    size = m_local * pieces
    first = got_ref.shape[0] - size
    count = first // 3
    shift = held_ref.shape[0] - got_ref.shape[0]
    components = (held_ref[:first] + got_ref[:first]).astype(jnp.int32)
    spectra = held_ref[first + shift :] + got_ref[first:]
    offsets = components[:count] - base
    amplitudes = (components[count : 2 * count], components[2 * count :])

    for local in range(m_local):
        offset = offsets - local * width
        group, place = offset // LANES, offset % LANES
        selected, places = [], []
        for line in range(count):
            here = group[line : line + 1] == lax.broadcasted_iota(jnp.int32, (groups, LANES), 0)
            column = []
            for amplitude in amplitudes:
                value = amplitude[line : line + 1]
                for part in (value // SPLIT, value % SPLIT):
                    column.append(jnp.where(here, part.astype(jnp.float32), 0.0))
            selected.append(jnp.concatenate(column, 0).astype(jnp.bfloat16))
            match = place[line : line + 1] == lax.broadcasted_iota(jnp.int32, (LANES, LANES), 0)
            places.append(jnp.where(match, 1.0, 0.0).astype(jnp.bfloat16))
        contract = (((1,), (1,)), ((), ()))
        counted = lax.dot_general(
            jnp.concatenate(selected, 1),
            jnp.concatenate(places, 1),
            contract,
            preferred_element_type=jnp.float32,
        ).astype(jnp.int32)
        model = []
        for part in range(2):
            high = counted[2 * part * groups : (2 * part + 1) * groups]
            low = counted[(2 * part + 1) * groups : (2 * part + 2) * groups]
            alm = (high * SPLIT + low).astype(jnp.float32) * UNIT
            model.append(jnp.concatenate([alm[g : g + 1] for g in range(groups)], 1))
        model_alm = jnp.concatenate(model, 0).astype(jnp.bfloat16)

        real_matrix, imag_matrix = transfer_ref[local, 0], transfer_ref[local, 1]
        by_real = lax.dot_general(model_alm, real_matrix, contract, preferred_element_type=jnp.float32)
        by_imag = lax.dot_general(model_alm, imag_matrix, contract, preferred_element_type=jnp.float32)
        pred_real = by_real[0:1] - by_imag[1:2]
        pred_imag = by_real[1:2] + by_imag[0:1]
        start = local * pieces
        spectrum = [
            jnp.concatenate([spectra[start + part * tiles + t : start + part * tiles + t + 1] for t in range(tiles)], 1)
            for part in range(2)
        ]
        resid_real = (spectrum[0] - pred_real).astype(jnp.bfloat16)
        resid_imag = (spectrum[1] - pred_imag).astype(jnp.bfloat16)
        with_real = jnp.concatenate([resid_real, resid_imag], 0)
        with_imag = jnp.concatenate([resid_imag, -resid_real], 0)
        out_ref[local] = jnp.dot(with_real, real_matrix, preferred_element_type=jnp.float32) + jnp.dot(
            with_imag, imag_matrix, preferred_element_type=jnp.float32
        )


def in_hbm(value):
    return pltpu.with_memory_space_constraint(value, pltpu.HBM)


def in_vmem(value):
    return pltpu.with_memory_space_constraint(value, pltpu.VMEM)


def swap(value, offset, devices):
    return lax.ppermute(value, "ma", [(device, device ^ offset) for device in range(devices)])


def body(vis, transfer, band_start, comp_index, comp_amp):
    devices = lax.axis_size("ma")
    samples, _, baselines = vis.shape
    m_local, _, _, width = transfer.shape
    comps = comp_index.shape[0]
    tiles = baselines // LANES
    pieces = 2 * tiles
    size = m_local * pieces
    first = 3 * padded(devices * slot_size(comps), LANES) // LANES
    rows = first + devices // 2 * size
    vmem, smem, hbm = (pl.BlockSpec(memory_space=space) for space in (pltpu.VMEM, pltpu.SMEM, pltpu.HBM))
    lines = vis.reshape(samples, 2, tiles, LANES).transpose(0, 2, 1, 3).reshape(samples * pieces, LANES)
    block = pltpu.VMEM((rows, LANES), jnp.float32)
    send, held, matrices = pl.pallas_call(
        functools.partial(transform_kernel, samples * devices, m_local * devices, m_local, comps),
        out_shape=(block, block, pltpu.VMEM(transfer.shape, transfer.dtype)),
        in_specs=[smem, hbm, hbm, hbm, hbm],
        out_specs=(vmem, vmem, vmem),
        scratch_shapes=[
            pltpu.VMEM((1, comps), jnp.int32),
            pltpu.VMEM((2, comps), jnp.int32),
            pltpu.VMEM(lines.shape, lines.dtype),
            pltpu.SemaphoreType.DMA((4,)),
        ],
        compiler_params=pltpu.CompilerParams(vmem_limit_bytes=VMEM_LIMIT),
        name="transform",
    )(band_start, in_hbm(lines), in_hbm(comp_index.reshape(1, comps)), in_hbm(comp_amp.T), in_hbm(transfer))
    offsets = offsets_of(devices)
    got = swap(send, offsets[0], devices)
    for step, offset in enumerate(offsets[1:], 1):
        shift = held.shape[0] - got.shape[0]
        summed = jnp.concatenate([held[:first] + got[:first], held[first + shift :] + got[first:]], 0)
        rows = first + (devices >> (step + 1)) * size
        held, got = summed, swap(summed[:rows], offset, devices)
    return pl.pallas_call(
        functools.partial(residual_kernel, m_local, pieces),
        out_shape=jax.ShapeDtypeStruct((m_local, 2, width), jnp.float32),
        in_specs=[vmem, vmem, vmem],
        out_specs=vmem,
        compiler_params=pltpu.CompilerParams(vmem_limit_bytes=VMEM_LIMIT),
        name="residual",
    )(in_vmem(held), in_vmem(got), in_vmem(matrices))


def solution(mesh):
    in_specs = (
        P(("grp", "ma"), None, None),
        P(("grp", "ma"), None, None, None),
        P("grp"),
        P(("grp", "ma")),
        P(("grp", "ma"), None),
    )
    out_specs = P(("grp", "ma"), None, None)
    return jax.shard_map(body, mesh=mesh, in_specs=in_specs, out_specs=out_specs, check_vma=False)
```

time: 18.3 us -> 17.3 us (0.945)
  blocking collectives: 14.1 us -> 0 us
  starting transfers between devices: 0 us -> 7.88 us
  waiting for transfers between devices: 0 us -> 5.22 us
    all_to_all x1 -> x0, blocking collectives: 14.1 us -> none  [body(): got = lax.all_to_all(send, 'ma', split_axis=0, concat_axis=0, tiled=True)]
    ppermute x0 -> x4, starting transfers between devices: none -> 7.88 us  [swap(): lax.ppermute(value, 'ma', [(device, device ^ offset) for device in range(...]
    ppermute x0 -> x4, waiting for transfers between devices: none -> 5.22 us  [swap(): lax.ppermute(value, 'ma', [(device, device ^ offset) for device in range(...]
  transfers between devices with their start and end apart: 0 -> 4, of which waited for: 0 -> 4; matrix products, arithmetic and copies ran while one was open for 0% -> 0% of each run, Pallas kernels for 0% -> 0%
where the time goes in v3:
time: 17.3 us; the launch traced here: 17.1 us
  starting transfers between devices  7.88 us (46%)
  waiting for transfers between devices  5.22 us (30%)
  Pallas kernels  3.31 us (19%)
  between operations  0.67 us (4%)
    ppermute x4, starting transfers between devices, swap(): lax.ppermute(value, 'ma', [(device, device ^ offset) for device in range(...  7.88 us
    ppermute x4, waiting for transfers between devices, swap(): lax.ppermute(value, 'ma', [(device, device ^ offset) for device in range(...  5.22 us
    pallas_call x1, Pallas kernels, body(): pl.pallas_call(functools.partial(transform_kernel, samples * devices, m_l...  1.69 us
    pallas_call x1, Pallas kernels, body(): pl.pallas_call(functools.partial(residual_kernel, m_local, pieces), out_s...  1.62 us
  transfers between devices with their start and end apart: 4, of which 4 were waited for; matrix products, arithmetic and copies ran while one was open for 0% of the time, Pallas kernels for 0%

profile of v3, /device:TPU:0, one launch (start us, length us, event | category | flops | bytes accessed | tf_op | source)
XLA Modules:
  0.0 17.1 jit_solution(3923864731340250833)
XLA Ops:
  0.7 1.7 %transform.1 = (f32[56,128]{1,0:T(8,128)S(1)}, f32[56,128]{1,0:T(8,128)S(1)}, bf16[1,2,256,1024]{3,2,1,0:T(8,128)(2,1)S(1)}) custom-call(s32[1]{0:T(128)S(6)} %copy.7.refs_0_, f32[2048,128]{1,0:T(8,128)} %bitcast.7, s32[1,64]{1,0:T(1,128)} %bitcast.9, s32[2,64]{1,0:T(2,128)} %bitcast.8, bf16[1,2,256,1024]{3,2,1,0:T(8,128)(2,1)} %refs_4_.1), custom_call_target="tpu_custom_call" | custom-call | tf_op jit(solution)/shard_map/transform/pallas_call | solution.py:210
  2.3 0.6 %collective-permute-start = (f32[56,128]{1,0:T(8,128)S(1)}, f32[56,128]{1,0:T(8,128)S(1)}, u32[]{:S(2)}, u32[]{:S(2)}) collective-permute-start(f32[56,128]{1,0:T(8,128)S(1)} %get-tuple-element.9), channel_id=1, source_target_pairs={{0,1},{1,0},{2,3},{3,2},{4,5},{5,4},{6,7},{7,6},{8,9},{9,8},{10,11... | collective-permute-start | bytes 86024 | tf_op jit(solution)/shard_map/ppermute | solution.py:194
  2.9 0.9 %collective-permute-done = f32[56,128]{1,0:T(8,128)S(1)} collective-permute-done((f32[56,128]{1,0:T(8,128)S(1)}, f32[56,128]{1,0:T(8,128)S(1)}, u32[]{:S(2)}, u32[]{:S(2)}) %collective-permute-start) | collective-permute-done | bytes 28704 | tf_op jit(solution)/shard_map/ppermute | solution.py:194
  3.8 2.7 %collective-permute-start.1 = (f32[40,128]{1,0:T(8,128)S(1)}, f32[40,128]{1,0:T(8,128)S(1)}, u32[]{:S(2)}, u32[]{:S(2)}) collective-permute-start(f32[40,128]{1,0:T(8,128)S(1)} %pad_maximum_fusion.1), channel_id=1, source_target_pairs={{0,3},{1,2},{2,1},{3,0},{4,7},{5,6},{6,5},{7,4},{8,11},{9,10},{10,... | collective-permute-start | bytes 61448 | tf_op jit(solution)/shard_map/ppermute | solution.py:194
  6.5 1.5 %collective-permute-done.1 = f32[40,128]{1,0:T(8,128)S(1)} collective-permute-done((f32[40,128]{1,0:T(8,128)S(1)}, f32[40,128]{1,0:T(8,128)S(1)}, u32[]{:S(2)}, u32[]{:S(2)}) %collective-permute-start.1) | collective-permute-done | bytes 20512 | tf_op jit(solution)/shard_map/ppermute | solution.py:194
  8.0 1.8 %collective-permute-start.2 = (f32[32,128]{1,0:T(8,128)S(1)}, f32[32,128]{1,0:T(8,128)S(1)}, u32[]{:S(2)}, u32[]{:S(2)}) collective-permute-start(f32[32,128]{1,0:T(8,128)S(1)} %pad_maximum_fusion.2), channel_id=1, source_target_pairs={{0,5},{1,4},{2,7},{3,6},{4,1},{5,0},{6,3},{7,2},{8,13},{9,12},{10,... | collective-permute-start | bytes 49160 | tf_op jit(solution)/shard_map/ppermute | solution.py:194
  9.8 1.4 %collective-permute-done.2 = f32[32,128]{1,0:T(8,128)S(1)} collective-permute-done((f32[32,128]{1,0:T(8,128)S(1)}, f32[32,128]{1,0:T(8,128)S(1)}, u32[]{:S(2)}, u32[]{:S(2)}) %collective-permute-start.2) | collective-permute-done | bytes 16416 | tf_op jit(solution)/shard_map/ppermute | solution.py:194
  11.3 2.8 %collective-permute-start.3 = (f32[28,128]{1,0:T(8,128)S(1)}, f32[28,128]{1,0:T(8,128)S(1)}, u32[]{:S(2)}, u32[]{:S(2)}) collective-permute-start(f32[28,128]{1,0:T(8,128)S(1)} %fusion), channel_id=1, source_target_pairs={{0,9},{1,8},{2,11},{3,10},{4,13},{5,12},{6,15},{7,14},{8,1},{9,0},... | collective-permute-start | bytes 43016 | tf_op jit(solution)/shard_map/ppermute | solution.py:194
  14.1 1.4 %collective-permute-done.3.got_ref = f32[28,128]{1,0:T(8,128)S(1)} collective-permute-done((f32[28,128]{1,0:T(8,128)S(1)}, f32[28,128]{1,0:T(8,128)S(1)}, u32[]{:S(2)}, u32[]{:S(2)}) %collective-permute-start.3) | collective-permute-done | bytes 14368 | tf_op jit(solution)/shard_map/ppermute | solution.py:194
  15.5 1.6 %residual.1 = f32[1,2,1024]{2,1,0:T(2,128)} custom-call(f32[32,128]{1,0:T(8,128)S(1)} %pad_maximum_fusion.held_ref, f32[28,128]{1,0:T(8,128)S(1)} %collective-permute-done.3.got_ref, bf16[1,2,256,1024]{3,2,1,0:T(8,128)(2,1)S(1)} %get-tuple-element.10.transfer_ref), custom_call_target="tpu_custom_call" | custom-call | tf_op jit(solution)/shard_map/residual/pallas_call | solution.py:231
  (10 shorter events, 0.0 us)
Async XLA Ops:
  2.3 1.4 %collective-permute-start = (f32[56,128]{1,0:T(8,128)S(1)}, f32[56,128]{1,0:T(8,128)S(1)}, u32[]{:S(2)}, u32[]{:S(2)}) collective-permute-start(f32[56,128]{1,0:T(8,128)S(1)} %get-tuple-element.9), channel_id=1, source_target_pairs={{0,1},{1,0},{2,3},{3,2},{4,5},{5,4},{6,7},{7,6},{8,9},{9,8},{10,11... | collective-permute-start | bytes 86024 | tf_op jit(solution)/shard_map/ppermute | solution.py:194
  3.8 4.2 %collective-permute-start.1 = (f32[40,128]{1,0:T(8,128)S(1)}, f32[40,128]{1,0:T(8,128)S(1)}, u32[]{:S(2)}, u32[]{:S(2)}) collective-permute-start(f32[40,128]{1,0:T(8,128)S(1)} %pad_maximum_fusion.1), channel_id=1, source_target_pairs={{0,3},{1,2},{2,1},{3,0},{4,7},{5,6},{6,5},{7,4},{8,11},{9,10},{10,... | collective-permute-start | bytes 61448 | tf_op jit(solution)/shard_map/ppermute | solution.py:194
  8.0 3.3 %collective-permute-start.2 = (f32[32,128]{1,0:T(8,128)S(1)}, f32[32,128]{1,0:T(8,128)S(1)}, u32[]{:S(2)}, u32[]{:S(2)}) collective-permute-start(f32[32,128]{1,0:T(8,128)S(1)} %pad_maximum_fusion.2), channel_id=1, source_target_pairs={{0,5},{1,4},{2,7},{3,6},{4,1},{5,0},{6,3},{7,2},{8,13},{9,12},{10,... | collective-permute-start | bytes 49160 | tf_op jit(solution)/shard_map/ppermute | solution.py:194
  11.3 4.2 %collective-permute-start.3 = (f32[28,128]{1,0:T(8,128)S(1)}, f32[28,128]{1,0:T(8,128)S(1)}, u32[]{:S(2)}, u32[]{:S(2)}) collective-permute-start(f32[28,128]{1,0:T(8,128)S(1)} %fusion), channel_id=1, source_target_pairs={{0,9},{1,8},{2,11},{3,10},{4,13},{5,12},{6,15},{7,14},{8,1},{9,0},... | collective-permute-start | bytes 43016 | tf_op jit(solution)/shard_map/ppermute | solution.py:194

commit v4 on v3

v4 whole, which is shorter than its diff:
```python
import functools
import math

import jax
import jax.numpy as jnp
from jax import lax
from jax.experimental import pallas as pl
from jax.experimental.pallas import tpu as pltpu
from jax.sharding import PartitionSpec as P

LANE_BITS = 7
LANES = 1 << LANE_BITS
SPLIT_BITS = 6
SPLIT = 1 << SPLIT_BITS
NT = (((1,), (1,)), ((), ()))
BLOCK = 256
UNIT = 1.0 / 1024.0
VMEM_LIMIT = 32 * 2**20
LEAD = 4 * 10**8


def padded(count, unit):
    return -(-count // unit) * unit


def cos_sin(phase, ticks):
    quarter = ticks // 4
    quadrant = (phase + quarter // 2) >> (quarter.bit_length() - 1)
    theta = (phase - quadrant * quarter).astype(jnp.float32) * (2.0 * math.pi / ticks)
    sq = theta * theta
    sine = theta * (1.0 + sq * (-1.0 / 6 + sq * (1.0 / 120 + sq * (-1.0 / 5040 + sq * (1.0 / 362880)))))
    cosine = 1.0 + sq * (-0.5 + sq * (1.0 / 24 + sq * (-1.0 / 720 + sq * (1.0 / 40320 - sq * (1.0 / 3628800)))))
    odd = (quadrant & 1) == 1
    cos_value = jnp.where(odd, sine, cosine)
    sin_value = jnp.where(odd, cosine, sine)
    cos_value = jnp.where(((quadrant + 1) & 2) == 2, -cos_value, cos_value)
    sin_value = jnp.where((quadrant & 2) == 2, -sin_value, sin_value)
    return cos_value, sin_value


def halves(value):
    high = value.astype(jnp.bfloat16)
    low = (value - high.astype(jnp.float32)).astype(jnp.bfloat16)
    return high, low


def offsets_of(devices):
    return [1] + [step | 1 for step in (1 << bit for bit in range(1, devices.bit_length() - 1))]


def tile_of(comps):
    lanes = LANES // 2 if comps <= LANES // 2 else LANES
    lines = -(-comps // lanes)
    parts = 4 * lanes // LANES
    return lanes, lines, parts, padded(3 * lines * parts, 8)


def table_kernel(ticks, m_local, *refs):
    band_ref, index_hbm, amp_hbm, table_ref, own_ref, index_ref, amp_ref, sems = refs
    copies = [
        pltpu.make_async_copy(index_hbm, index_ref, sems.at[0]),
        pltpu.make_async_copy(amp_hbm, amp_ref, sems.at[1]),
    ]
    for copy in copies:
        copy.start()
    rank = lax.axis_index("ma")
    modes, samples = table_ref.shape[0] // 4, table_ref.shape[1]
    devices = modes // m_local
    row = lax.broadcasted_iota(jnp.int32, (modes, samples), 0)
    position = row % devices
    receiver = jnp.broadcast_to(rank, (modes, samples))
    for step, offset in enumerate(offsets_of(devices)):
        receiver ^= jnp.where((position & (devices >> (step + 1))) == 0, offset, 0)
    order = band_ref[0] + receiver * m_local + row // devices
    moment = rank * samples + lax.broadcasted_iota(jnp.int32, (modes, samples), 1)
    values = [halves(value) for value in cos_sin((order * moment) & (ticks - 1), ticks)]
    for part in range(4):
        table_ref[part * modes : (part + 1) * modes] = values[part % 2][part // 2]

    comps = index_ref.shape[1]
    lanes, lines, parts, _ = tile_of(comps)
    own_ref[...] = jnp.zeros(own_ref.shape, jnp.float32)
    shared = LANES // lanes
    mine = lax.broadcasted_iota(jnp.int32, (1, LANES), 1) // lanes == rank % shared
    start = 3 * lines * (rank % 4 // shared)
    for copy in copies:
        copy.wait()
    for which in range(3):
        source = index_ref[...] if which == 0 else amp_ref[which - 1 : which, :]
        for line in range(lines):
            value = source[:, line * lanes : (line + 1) * lanes].astype(jnp.float32)
            if value.shape[1] < lanes:
                value = jnp.concatenate([value, jnp.zeros((1, lanes - value.shape[1]), jnp.float32)], 1)
            value = jnp.where(mine, jnp.concatenate([value] * shared, 1), 0.0)
            own_ref[pl.ds(start + which * lines + line, 1), :] = value


def transform_kernel(ticks, m_local, table_ref, vis_ref, own_ref, send_ref, keep_ref):
    modes, samples = table_ref.shape[0] // 4, table_ref.shape[1]
    devices = modes // m_local
    pieces = vis_ref.shape[0] // samples
    tiles = pieces // 2
    half, size = devices // 2, m_local * pieces
    first = own_ref.shape[0]
    send_ref[:first] = own_ref[...]
    keep_ref[:first] = own_ref[...]
    scale = 1.0 / math.sqrt(ticks)
    for tile in range(tiles):
        parts = [vis_ref[pl.ds(tile * 2 + part, samples, stride=pieces), :] for part in range(2)]
        high, low = halves(jnp.concatenate(parts, 1))
        product = jnp.dot(table_ref[...], high, preferred_element_type=jnp.float32)
        product += jnp.dot(table_ref[...], low, preferred_element_type=jnp.float32)
        product = product[: 2 * modes] + product[2 * modes :]
        from_cos, from_sin = product[:modes], product[modes:]
        real_part = (from_cos[:, :LANES] + from_sin[:, LANES:]) * scale
        imag_part = (from_cos[:, LANES:] - from_sin[:, :LANES]) * scale
        for local in range(m_local):
            for part, value in enumerate((real_part, imag_part)):
                start = first + local * pieces + part * tiles + tile
                at = local * devices
                send_ref[pl.ds(start, half, stride=size), :] = value[at : at + half]
                keep_ref[pl.ds(start, half, stride=size), :] = value[at + half : at + devices]


def fetch_kernel(after_ref, transfer_hbm, transfer_ref, sem):
    copy = pltpu.make_async_copy(transfer_hbm, transfer_ref, sem)
    copy.start()
    copy.wait()


def counts_of(components, comps, base, groups):
    lanes, lines, parts, rows = tile_of(comps)
    numbers = components.astype(jnp.int32)
    group, place = (numbers - base) >> LANE_BITS, (numbers - base) & (LANES - 1)
    high, low = (numbers >> SPLIT_BITS).astype(jnp.float32), (numbers & (SPLIT - 1)).astype(jnp.float32)
    slot = lax.broadcasted_iota(jnp.int32, (groups, LANES), 0)
    lane = lax.broadcasted_iota(jnp.int32, (LANES, LANES), 0)
    selected, places = [], []
    for tile in range(components.shape[0] // rows):
        for part in range(parts):
            for line in range(lines):
                at = tile * rows + 3 * lines * part + line
                here = group[at : at + 1] == slot
                column = []
                for field in (at + lines, at + 2 * lines):
                    column += [jnp.where(here, value[field : field + 1], 0.0) for value in (high, low)]
                selected.append(jnp.concatenate(column, 0).astype(jnp.bfloat16))
                places.append(jnp.where(place[at : at + 1] == lane, 1.0, 0.0).astype(jnp.bfloat16))
    return lax.dot_general(
        jnp.concatenate(selected, 1), jnp.concatenate(places, 1), NT, preferred_element_type=jnp.float32
    )


def count_kernel(m_local, width, comps, held_ref, count_ref):
    groups = width // LANES
    first = held_ref.shape[0]
    for local in range(m_local):
        base = (lax.axis_index("ma") * m_local + local) * width
        count_ref[local] = counts_of(held_ref[...], comps, base, groups)


def residual_kernel(m_local, pieces, comps, count_ref, held_ref, got_ref, transfer_ref, out_ref):
    width = transfer_ref.shape[3]
    tiles = pieces // 2
    groups = width // LANES
    size = m_local * pieces
    first = got_ref.shape[0] - size
    spectra = held_ref[...] + got_ref[first:]
    for local in range(m_local):
        base = (lax.axis_index("ma") * m_local + local) * width
        counted = (count_ref[local] + counts_of(got_ref[:first], comps, base, groups)).astype(jnp.int32)
        model = []
        for part in range(2):
            high = counted[2 * part * groups : (2 * part + 1) * groups]
            low = counted[(2 * part + 1) * groups : (2 * part + 2) * groups]
            alm = ((high << SPLIT_BITS) + low).astype(jnp.float32) * UNIT
            model.append(jnp.concatenate([alm[g : g + 1] for g in range(groups)], 1))
        model_alm = jnp.concatenate(model, 0).astype(jnp.bfloat16)

        real_matrix, imag_matrix = transfer_ref[local, 0], transfer_ref[local, 1]
        by_real = lax.dot_general(model_alm, real_matrix, NT, preferred_element_type=jnp.float32)
        by_imag = lax.dot_general(model_alm, imag_matrix, NT, preferred_element_type=jnp.float32)
        pred_real = by_real[0:1] - by_imag[1:2]
        pred_imag = by_real[1:2] + by_imag[0:1]
        start = local * pieces
        spectrum = [
            jnp.concatenate([spectra[start + part * tiles + t : start + part * tiles + t + 1] for t in range(tiles)], 1)
            for part in range(2)
        ]
        resid_real = (spectrum[0] - pred_real).astype(jnp.bfloat16)
        resid_imag = (spectrum[1] - pred_imag).astype(jnp.bfloat16)
        with_real = jnp.concatenate([resid_real, resid_imag], 0)
        with_imag = jnp.concatenate([resid_imag, -resid_real], 0)
        for column in range(0, width, BLOCK):
            block = slice(column, column + BLOCK)
            out_ref[local, :, block] = jnp.dot(
                with_real, real_matrix[:, block], preferred_element_type=jnp.float32
            ) + jnp.dot(with_imag, imag_matrix[:, block], preferred_element_type=jnp.float32)


def in_hbm(value):
    return pltpu.with_memory_space_constraint(value, pltpu.HBM)


def in_vmem(value):
    return pltpu.with_memory_space_constraint(value, pltpu.VMEM)


def swap(value, offset, devices):
    return lax.ppermute(value, "ma", [(device, device ^ offset) for device in range(devices)])


def body(vis, transfer, band_start, comp_index, comp_amp):
    devices = lax.axis_size("ma")
    samples, _, baselines = vis.shape
    m_local, _, _, width = transfer.shape
    comps = comp_index.shape[0]
    tiles = baselines // LANES
    pieces = 2 * tiles
    size = m_local * pieces
    unit = tile_of(comps)[3]
    vmem, smem, hbm = (pl.BlockSpec(memory_space=space) for space in (pltpu.VMEM, pltpu.SMEM, pltpu.HBM))
    params = pltpu.CompilerParams(vmem_limit_bytes=VMEM_LIMIT)
    lines = vis.reshape(samples, 2, tiles, LANES).transpose(0, 2, 1, 3).reshape(samples * pieces, LANES)
    table, own = pl.pallas_call(
        functools.partial(table_kernel, samples * devices, m_local),
        out_shape=(
            pltpu.VMEM((4 * m_local * devices, samples), jnp.bfloat16),
            pltpu.VMEM((unit, LANES), jnp.float32),
        ),
        in_specs=[smem, hbm, hbm],
        out_specs=(vmem, vmem),
        scratch_shapes=[
            pltpu.VMEM((1, comps), jnp.int32),
            pltpu.VMEM((2, comps), jnp.int32),
            pltpu.SemaphoreType.DMA((2,)),
        ],
        compiler_params=params,
        cost_estimate=pl.CostEstimate(flops=LEAD, transcendentals=0, bytes_accessed=0),
        name="table",
    )(band_start, in_hbm(comp_index.reshape(1, comps)), in_hbm(comp_amp.T))
    part = pltpu.VMEM((unit + devices // 2 * size, LANES), jnp.float32)
    send, keep = pl.pallas_call(
        functools.partial(transform_kernel, samples * devices, m_local),
        out_shape=(part, part),
        in_specs=[vmem, vmem, vmem],
        out_specs=(vmem, vmem),
        compiler_params=params,
        name="transform",
    )(in_vmem(table), in_vmem(lines), in_vmem(own))
    offsets = offsets_of(devices)
    got = swap(send, offsets[0], devices)
    components, spectra = keep[:unit], keep[unit:]
    for step, offset in enumerate(offsets[1:], 1):
        first = got.shape[0] - spectra.shape[0]
        if step <= 2:
            components = components + got[:first]
        else:
            components = jnp.concatenate([components, got[:first]], 0)
        spectra = spectra + got[first:]
        going = spectra.shape[0] // 2
        send = jnp.concatenate([components, spectra[:going]], 0)
        if step == 1:
            matrices = pl.pallas_call(
                fetch_kernel,
                out_shape=pltpu.VMEM(transfer.shape, transfer.dtype),
                in_specs=[vmem, hbm],
                out_specs=vmem,
                scratch_shapes=[pltpu.SemaphoreType.DMA],
                compiler_params=params,
                name="fetch",
            )(in_vmem(send), in_hbm(transfer))
        got, spectra = swap(send, offset, devices), spectra[going:]
    count = pl.pallas_call(
        functools.partial(count_kernel, m_local, width, comps),
        out_shape=pltpu.VMEM((m_local, 4 * width // LANES, LANES), jnp.float32),
        in_specs=[vmem],
        out_specs=vmem,
        compiler_params=params,
        name="count",
    )(in_vmem(components))
    return pl.pallas_call(
        functools.partial(residual_kernel, m_local, pieces, comps),
        out_shape=jax.ShapeDtypeStruct((m_local, 2, width), jnp.float32),
        in_specs=[vmem, vmem, vmem, vmem],
        out_specs=vmem,
        compiler_params=params,
        name="residual",
    )(in_vmem(count), in_vmem(spectra), in_vmem(got), in_vmem(matrices))


def solution(mesh):
    in_specs = (
        P(("grp", "ma"), None, None),
        P(("grp", "ma"), None, None, None),
        P("grp"),
        P(("grp", "ma")),
        P(("grp", "ma"), None),
    )
    out_specs = P(("grp", "ma"), None, None)
    return jax.shard_map(body, mesh=mesh, in_specs=in_specs, out_specs=out_specs, check_vma=False)
```

time: 17.3 us -> 16.3 us (0.942)
  waiting for transfers between devices: 5.22 us -> 3.62 us
  Pallas kernels: 3.31 us -> 3.8 us
    pallas_call x1 -> x4, Pallas kernels: 1.62 us -> 3.48 us  [the longest x1 1.31 us: body(): pl.pallas_call(functools.partial(residual_kernel, m_local, pieces, comps)...]
    ppermute x4, waiting for transfers between devices: 5.22 us -> 3.62 us  [swap(): lax.ppermute(value, 'ma', [(device, device ^ offset) for device in range(...]
    pallas_call x1, Pallas kernels: 1.69 us -> 0.31 us  [body(): pl.pallas_call(functools.partial(transform_kernel, samples * devices, m_l...]
  transfers between devices with their start and end apart: 4 -> 4, of which waited for: 4 -> 4; matrix products, arithmetic and copies ran while one was open for 0% -> 0% of each run, Pallas kernels for 0% -> 9%
where the time goes in v4:
time: 16.3 us; the launch traced here: 16.1 us
  starting transfers between devices  7.84 us (48%)
  Pallas kernels  3.8 us (23%)
  waiting for transfers between devices  3.62 us (22%)
  between operations  0.79 us (5%)
    ppermute x4, starting transfers between devices, swap(): lax.ppermute(value, 'ma', [(device, device ^ offset) for device in range(...  7.84 us
    ppermute x4, waiting for transfers between devices, swap(): lax.ppermute(value, 'ma', [(device, device ^ offset) for device in range(...  3.62 us
    pallas_call x1, Pallas kernels, body(): pl.pallas_call(functools.partial(residual_kernel, m_local, pieces, comps)...  1.31 us
    pallas_call x1, Pallas kernels, body(): pl.pallas_call(fetch_kernel, out_shape=pltpu.VMEM(transfer.shape, transfe...  1.23 us
    pallas_call x1, Pallas kernels, body(): pl.pallas_call(functools.partial(table_kernel, samples * devices, m_local...  0.79 us
  transfers between devices with their start and end apart: 4, of which 4 were waited for; matrix products, arithmetic and copies ran while one was open for 0% of the time, Pallas kernels for 9%

profile of v4, /device:TPU:0, one launch (start us, length us, event | category | flops | bytes accessed | tf_op | source)
XLA Modules:
  0.0 16.1 jit_solution(5344446058354641483)
XLA Ops:
  0.0 0.0 copy-start
  0.7 0.8 %table.1 = (bf16[64,512]{1,0:T(8,128)(2,1)S(1)}, f32[8,128]{1,0:T(8,128)S(1)}) custom-call(s32[1]{0:T(128)S(6)} %copy.7.refs_0_, s32[1,64]{1,0:T(1,128)} %bitcast.9, s32[2,64]{1,0:T(2,128)} %bitcast.8), custom_call_target="tpu_custom_call" | custom-call | flops 400000000 | tf_op jit(solution)/shard_map/table/pallas_call | solution.py:225
  1.5 0.0 copy-done
  1.5 0.3 %transform.1 = (f32[40,128]{1,0:T(8,128)S(1)}, f32[40,128]{1,0:T(8,128)S(1)}) custom-call(bf16[64,512]{1,0:T(8,128)(2,1)S(1)} %get-tuple-element.9.table_ref, f32[2048,128]{1,0:T(8,128)S(1)} %bitcast.7, f32[8,128]{1,0:T(8,128)S(1)} %get-tuple-element.10.own_ref), custom_call_target="tpu_custom_call" | custom-call | tf_op jit(solution)/shard_map/transform/pallas_call | solution.py:243
  1.9 0.5 %collective-permute-start = (f32[40,128]{1,0:T(8,128)S(1)}, f32[40,128]{1,0:T(8,128)S(1)}, u32[]{:S(2)}, u32[]{:S(2)}) collective-permute-start(f32[40,128]{1,0:T(8,128)S(1)} %get-tuple-element.12), channel_id=1, source_target_pairs={{0,1},{1,0},{2,3},{3,2},{4,5},{5,4},{6,7},{7,6},{8,9},{9,8},{10,11... | collective-permute-start | bytes 61448 | tf_op jit(solution)/shard_map/ppermute | solution.py:210
  2.4 0.8 %collective-permute-done = f32[40,128]{1,0:T(8,128)S(1)} collective-permute-done((f32[40,128]{1,0:T(8,128)S(1)}, f32[40,128]{1,0:T(8,128)S(1)}, u32[]{:S(2)}, u32[]{:S(2)}) %collective-permute-start) | collective-permute-done | bytes 20512 | tf_op jit(solution)/shard_map/ppermute | solution.py:210
  3.3 2.7 %collective-permute-start.1 = (f32[24,128]{1,0:T(8,128)S(1)}, f32[24,128]{1,0:T(8,128)S(1)}, u32[]{:S(2)}, u32[]{:S(2)}) collective-permute-start(f32[24,128]{1,0:T(8,128)S(1)} %pad_maximum_fusion.after_ref), channel_id=1, source_target_pairs={{0,3},{1,2},{2,1},{3,0},{4,7},{5,6},{6,5},{7,4},{8,11},{9,10},{10,... | collective-permute-start | bytes 36872 | tf_op jit(solution)/shard_map/ppermute | solution.py:210
  5.9 1.4 %collective-permute-done.1 = f32[24,128]{1,0:T(8,128)S(1)} collective-permute-done((f32[24,128]{1,0:T(8,128)S(1)}, f32[24,128]{1,0:T(8,128)S(1)}, u32[]{:S(2)}, u32[]{:S(2)}) %collective-permute-start.1) | collective-permute-done | bytes 12320 | tf_op jit(solution)/shard_map/ppermute | solution.py:210
  7.4 1.8 %collective-permute-start.2 = (f32[16,128]{1,0:T(8,128)S(1)}, f32[16,128]{1,0:T(8,128)S(1)}, u32[]{:S(2)}, u32[]{:S(2)}) collective-permute-start(f32[16,128]{1,0:T(8,128)S(1)} %pad_maximum_fusion.2), channel_id=1, source_target_pairs={{0,5},{1,4},{2,7},{3,6},{4,1},{5,0},{6,3},{7,2},{8,13},{9,12},{10,... | collective-permute-start | bytes 24584 | tf_op jit(solution)/shard_map/ppermute | solution.py:210
  9.2 1.2 %fetch.1.transfer_ref = bf16[1,2,256,1024]{3,2,1,0:T(8,128)(2,1)S(1)} custom-call(f32[24,128]{1,0:T(8,128)S(1)} %pad_maximum_fusion.after_ref, bf16[1,2,256,1024]{3,2,1,0:T(8,128)(2,1)} %transfer_hbm.1), custom_call_target="tpu_custom_call" | custom-call | tf_op jit(solution)/shard_map/fetch/pallas_call | solution.py:264
  10.5 0.1 collective-permute-done.2
  10.6 2.8 %collective-permute-start.3 = (f32[20,128]{1,0:T(8,128)S(1)}, f32[20,128]{1,0:T(8,128)S(1)}, u32[]{:S(2)}, u32[]{:S(2)}) collective-permute-start(f32[20,128]{1,0:T(8,128)S(1)} %pad_maximum_fusion.1), channel_id=1, source_target_pairs={{0,9},{1,8},{2,11},{3,10},{4,13},{5,12},{6,15},{7,14},{8,1},{9,0},... | collective-permute-start | bytes 30728 | tf_op jit(solution)/shard_map/ppermute | solution.py:210
  13.4 0.2 count.1.count_ref
  13.5 1.2 %collective-permute-done.3.got_ref = f32[20,128]{1,0:T(8,128)S(1)} collective-permute-done((f32[20,128]{1,0:T(8,128)S(1)}, f32[20,128]{1,0:T(8,128)S(1)}, u32[]{:S(2)}, u32[]{:S(2)}) %collective-permute-start.3) | collective-permute-done | bytes 10272 | tf_op jit(solution)/shard_map/ppermute | solution.py:210
  14.8 1.3 %residual.1 = f32[1,2,1024]{2,1,0:T(2,128)} custom-call(f32[1,32,128]{2,1,0:T(8,128)S(1)} %count.1.count_ref, f32[4,128]{1,0:T(4,128)S(1)} %get-tuple-element.16.held_ref, f32[20,128]{1,0:T(8,128)S(1)} %collective-permute-done.3.got_ref, bf16[1,2,256,1024]{3,2,1,0:T(8,128)(2,1)S(1)} %fetch.1.transfer_ref), custom_call_target="tpu_custom_call" | custom-call | tf_op jit(solution)/shard_map/residual/pallas_call | solution.py:282
  (12 shorter events, 0.1 us)
Async XLA Ops:
  0.0 1.5 %copy-start = (f32[512,2,256]{2,1,0:T(2,128)S(1)}, f32[512,2,256]{2,1,0:T(2,128)}, u32[]{:S(2)}) copy-start(f32[512,2,256]{2,1,0:T(2,128)} %param.5) | copy-start | bytes 3145732
  1.9 1.4 %collective-permute-start = (f32[40,128]{1,0:T(8,128)S(1)}, f32[40,128]{1,0:T(8,128)S(1)}, u32[]{:S(2)}, u32[]{:S(2)}) collective-permute-start(f32[40,128]{1,0:T(8,128)S(1)} %get-tuple-element.12), channel_id=1, source_target_pairs={{0,1},{1,0},{2,3},{3,2},{4,5},{5,4},{6,7},{7,6},{8,9},{9,8},{10,11... | collective-permute-start | bytes 61448 | tf_op jit(solution)/shard_map/ppermute | solution.py:210
  3.3 4.1 %collective-permute-start.1 = (f32[24,128]{1,0:T(8,128)S(1)}, f32[24,128]{1,0:T(8,128)S(1)}, u32[]{:S(2)}, u32[]{:S(2)}) collective-permute-start(f32[24,128]{1,0:T(8,128)S(1)} %pad_maximum_fusion.after_ref), channel_id=1, source_target_pairs={{0,3},{1,2},{2,1},{3,0},{4,7},{5,6},{6,5},{7,4},{8,11},{9,10},{10,... | collective-permute-start | bytes 36872 | tf_op jit(solution)/shard_map/ppermute | solution.py:210
  7.4 3.2 %collective-permute-start.2 = (f32[16,128]{1,0:T(8,128)S(1)}, f32[16,128]{1,0:T(8,128)S(1)}, u32[]{:S(2)}, u32[]{:S(2)}) collective-permute-start(f32[16,128]{1,0:T(8,128)S(1)} %pad_maximum_fusion.2), channel_id=1, source_target_pairs={{0,5},{1,4},{2,7},{3,6},{4,1},{5,0},{6,3},{7,2},{8,13},{9,12},{10,... | collective-permute-start | bytes 24584 | tf_op jit(solution)/shard_map/ppermute | solution.py:210
  10.6 4.2 %collective-permute-start.3 = (f32[20,128]{1,0:T(8,128)S(1)}, f32[20,128]{1,0:T(8,128)S(1)}, u32[]{:S(2)}, u32[]{:S(2)}) collective-permute-start(f32[20,128]{1,0:T(8,128)S(1)} %pad_maximum_fusion.1), channel_id=1, source_target_pairs={{0,9},{1,8},{2,11},{3,10},{4,13},{5,12},{6,15},{7,14},{8,1},{9,0},... | collective-permute-start | bytes 30728 | tf_op jit(solution)/shard_map/ppermute | solution.py:210

commit v5 on v4

--- a/solution.py
+++ b/solution.py
@@ -16,7 +16,7 @@
 BLOCK = 256
 UNIT = 1.0 / 1024.0
 VMEM_LIMIT = 32 * 2**20
-LEAD = 4 * 10**8
+LEAD = 400000000
 
 
 def padded(count, unit):
@@ -55,14 +55,7 @@
     return lanes, lines, parts, padded(3 * lines * parts, 8)
 
 
-def table_kernel(ticks, m_local, *refs):
-    band_ref, index_hbm, amp_hbm, table_ref, own_ref, index_ref, amp_ref, sems = refs
-    copies = [
-        pltpu.make_async_copy(index_hbm, index_ref, sems.at[0]),
-        pltpu.make_async_copy(amp_hbm, amp_ref, sems.at[1]),
-    ]
-    for copy in copies:
-        copy.start()
+def table_kernel(ticks, m_local, band_ref, table_ref):
     rank = lax.axis_index("ma")
     modes, samples = table_ref.shape[0] // 4, table_ref.shape[1]
     devices = modes // m_local
@@ -77,33 +70,47 @@
     for part in range(4):
         table_ref[part * modes : (part + 1) * modes] = values[part % 2][part // 2]
 
+
+def pack_kernel(after_ref, index_hbm, amp_hbm, index_other_ref, amp_other_ref, tile_ref, index_ref, amp_ref, sems):
+    copies = [
+        pltpu.make_async_copy(index_hbm, index_ref, sems.at[0]),
+        pltpu.make_async_copy(amp_hbm, amp_ref, sems.at[1]),
+    ]
+    for copy in copies:
+        copy.start()
     comps = index_ref.shape[1]
-    lanes, lines, parts, _ = tile_of(comps)
-    own_ref[...] = jnp.zeros(own_ref.shape, jnp.float32)
+    lanes, lines, _, _ = tile_of(comps)
     shared = LANES // lanes
-    mine = lax.broadcasted_iota(jnp.int32, (1, LANES), 1) // lanes == rank % shared
-    start = 3 * lines * (rank % 4 // shared)
+    tile_ref[...] = jnp.zeros(tile_ref.shape, jnp.float32)
     for copy in copies:
         copy.wait()
+    lane = lax.broadcasted_iota(jnp.int32, (1, LANES), 1) // lanes
+    own = lax.axis_index("ma")
+    other = own ^ 1
     for which in range(3):
-        source = index_ref[...] if which == 0 else amp_ref[which - 1 : which, :]
         for line in range(lines):
-            value = source[:, line * lanes : (line + 1) * lanes].astype(jnp.float32)
-            if value.shape[1] < lanes:
-                value = jnp.concatenate([value, jnp.zeros((1, lanes - value.shape[1]), jnp.float32)], 1)
-            value = jnp.where(mine, jnp.concatenate([value] * shared, 1), 0.0)
-            own_ref[pl.ds(start + which * lines + line, 1), :] = value
-
-
-def transform_kernel(ticks, m_local, table_ref, vis_ref, own_ref, send_ref, keep_ref):
+            rows = []
+            for index, amp in ((index_ref, amp_ref), (index_other_ref, amp_other_ref)):
+                source = index[...] if which == 0 else amp[which - 1 : which, :]
+                value = source[:, line * lanes : (line + 1) * lanes].astype(jnp.float32)
+                if value.shape[1] < lanes:
+                    value = jnp.concatenate([value, jnp.zeros((1, lanes - value.shape[1]), jnp.float32)], 1)
+                rows.append(jnp.concatenate([value] * shared, 1))
+            place = which * lines + line
+            if shared == 2:
+                value = jnp.where(lane == own % 2, rows[0], rows[1])
+                tile_ref[pl.ds(3 * lines * (own % 4 // 2) + place, 1), :] = value
+            else:
+                tile_ref[pl.ds(3 * lines * (own % 4) + place, 1), :] = rows[0]
+                tile_ref[pl.ds(3 * lines * (other % 4) + place, 1), :] = rows[1]
+
+
+def transform_kernel(ticks, m_local, table_ref, vis_ref, send_ref, keep_ref):
     modes, samples = table_ref.shape[0] // 4, table_ref.shape[1]
     devices = modes // m_local
     pieces = vis_ref.shape[0] // samples
     tiles = pieces // 2
     half, size = devices // 2, m_local * pieces
-    first = own_ref.shape[0]
-    send_ref[:first] = own_ref[...]
-    keep_ref[:first] = own_ref[...]
     scale = 1.0 / math.sqrt(ticks)
     for tile in range(tiles):
         parts = [vis_ref[pl.ds(tile * 2 + part, samples, stride=pieces), :] for part in range(2)]
@@ -116,7 +123,7 @@
         imag_part = (from_cos[:, LANES:] - from_sin[:, :LANES]) * scale
         for local in range(m_local):
             for part, value in enumerate((real_part, imag_part)):
-                start = first + local * pieces + part * tiles + tile
+                start = local * pieces + part * tiles + tile
                 at = local * devices
                 send_ref[pl.ds(start, half, stride=size), :] = value[at : at + half]
                 keep_ref[pl.ds(start, half, stride=size), :] = value[at + half : at + devices]
@@ -129,7 +136,7 @@
 
 
 def counts_of(components, comps, base, groups):
-    lanes, lines, parts, rows = tile_of(comps)
+    _, lines, parts, rows = tile_of(comps)
     numbers = components.astype(jnp.int32)
     group, place = (numbers - base) >> LANE_BITS, (numbers - base) & (LANES - 1)
     high, low = (numbers >> SPLIT_BITS).astype(jnp.float32), (numbers & (SPLIT - 1)).astype(jnp.float32)
@@ -153,7 +160,6 @@
 
 def count_kernel(m_local, width, comps, held_ref, count_ref):
     groups = width // LANES
-    first = held_ref.shape[0]
     for local in range(m_local):
         base = (lax.axis_index("ma") * m_local + local) * width
         count_ref[local] = counts_of(held_ref[...], comps, base, groups)
@@ -222,40 +228,47 @@
     vmem, smem, hbm = (pl.BlockSpec(memory_space=space) for space in (pltpu.VMEM, pltpu.SMEM, pltpu.HBM))
     params = pltpu.CompilerParams(vmem_limit_bytes=VMEM_LIMIT)
     lines = vis.reshape(samples, 2, tiles, LANES).transpose(0, 2, 1, 3).reshape(samples * pieces, LANES)
-    table, own = pl.pallas_call(
+    offsets = offsets_of(devices)
+    index, amp = comp_index.reshape(1, comps), comp_amp.T
+    index_other = swap(comp_index, offsets[0], devices).reshape(1, comps)
+    amp_other = swap(comp_amp, offsets[0], devices).T
+    table = pl.pallas_call(
         functools.partial(table_kernel, samples * devices, m_local),
-        out_shape=(
-            pltpu.VMEM((4 * m_local * devices, samples), jnp.bfloat16),
-            pltpu.VMEM((unit, LANES), jnp.float32),
-        ),
-        in_specs=[smem, hbm, hbm],
+        out_shape=pltpu.VMEM((4 * m_local * devices, samples), jnp.bfloat16),
+        in_specs=[smem],
+        out_specs=vmem,
+        compiler_params=params,
+        cost_estimate=pl.CostEstimate(flops=LEAD, transcendentals=0, bytes_accessed=0),
+        name="table",
+    )(band_start)
+    part = pltpu.VMEM((devices // 2 * size, LANES), jnp.float32)
+    send, spectra = pl.pallas_call(
+        functools.partial(transform_kernel, samples * devices, m_local),
+        out_shape=(part, part),
+        in_specs=[vmem, vmem],
         out_specs=(vmem, vmem),
+        compiler_params=params,
+        name="transform",
+    )(in_vmem(table), in_vmem(lines))
+    components = pl.pallas_call(
+        pack_kernel,
+        out_shape=pltpu.VMEM((unit, LANES), jnp.float32),
+        in_specs=[vmem, hbm, hbm, vmem, vmem],
+        out_specs=vmem,
         scratch_shapes=[
             pltpu.VMEM((1, comps), jnp.int32),
             pltpu.VMEM((2, comps), jnp.int32),
             pltpu.SemaphoreType.DMA((2,)),
         ],
         compiler_params=params,
-        cost_estimate=pl.CostEstimate(flops=LEAD, transcendentals=0, bytes_accessed=0),
-        name="table",
-    )(band_start, in_hbm(comp_index.reshape(1, comps)), in_hbm(comp_amp.T))
-    part = pltpu.VMEM((unit + devices // 2 * size, LANES), jnp.float32)
-    send, keep = pl.pallas_call(
-        functools.partial(transform_kernel, samples * devices, m_local),
-        out_shape=(part, part),
-        in_specs=[vmem, vmem, vmem],
-        out_specs=(vmem, vmem),
-        compiler_params=params,
-        name="transform",
-    )(in_vmem(table), in_vmem(lines), in_vmem(own))
-    offsets = offsets_of(devices)
+        name="pack",
+    )(in_vmem(spectra), in_hbm(index), in_hbm(amp), in_vmem(index_other), in_vmem(amp_other))
     got = swap(send, offsets[0], devices)
-    components, spectra = keep[:unit], keep[unit:]
     for step, offset in enumerate(offsets[1:], 1):
         first = got.shape[0] - spectra.shape[0]
-        if step <= 2:
+        if step == 2:
             components = components + got[:first]
-        else:
+        elif step > 2:
             components = jnp.concatenate([components, got[:first]], 0)
         spectra = spectra + got[first:]
         going = spectra.shape[0] // 2

time: 16.3 us -> 17.8 us (1.092)
  local copies, waits for them, and re-layouts: 0.02 us -> 0.59 us
  starting transfers between devices: 7.84 us -> 8.37 us
  waiting for transfers between devices: 3.62 us -> 3.93 us
    pallas_call x0 -> x1, Pallas kernels: none -> 0.79 us  [body(): pl.pallas_call(pack_kernel, out_shape=pltpu.VMEM((unit, LANES), jnp.float...]
    pallas_call x1, Pallas kernels: 0.79 us -> 0.07 us  [body(): pl.pallas_call(functools.partial(table_kernel, samples * devices, m_local...]
    unnamed x2 -> x6, local copies, waits for them, and re-layouts: 0.01 us -> 0.57 us
    ppermute x4 -> x6, starting transfers between devices: 7.84 us -> 8.37 us  [swap(): lax.ppermute(value, 'ma', [(device, device ^ offset) for device in range(...]
    ppermute x4 -> x6, waiting for transfers between devices: 3.62 us -> 3.93 us  [swap(): lax.ppermute(value, 'ma', [(device, device ^ offset) for device in range(...]
  transfers between devices with their start and end apart: 4 -> 6, of which waited for: 4 -> 4; matrix products, arithmetic and copies ran while one was open for 0% -> 0% of each run, Pallas kernels for 9% -> 12%
where the time goes in v5:
time: 17.8 us; the launch traced here: 17.6 us
  starting transfers between devices  8.37 us (47%)
  waiting for transfers between devices  3.93 us (22%)
  Pallas kernels  3.86 us (22%)
  between operations  0.83 us (5%)
  local copies, waits for them, and re-layouts  0.59 us (3%)
    ppermute x6, starting transfers between devices, swap(): lax.ppermute(value, 'ma', [(device, device ^ offset) for device in range(...  8.37 us
    ppermute x6, waiting for transfers between devices, swap(): lax.ppermute(value, 'ma', [(device, device ^ offset) for device in range(...  3.93 us
    pallas_call x1, Pallas kernels, body(): pl.pallas_call(functools.partial(residual_kernel, m_local, pieces, comps)...  1.31 us
    pallas_call x1, Pallas kernels, body(): pl.pallas_call(fetch_kernel, out_shape=pltpu.VMEM(transfer.shape, transfe...  1.23 us
    pallas_call x1, Pallas kernels, body(): pl.pallas_call(pack_kernel, out_shape=pltpu.VMEM((unit, LANES), jnp.float...  0.79 us
    unnamed x6, local copies, waits for them, and re-layouts  0.57 us
  transfers between devices with their start and end apart: 6, of which 4 were waited for; matrix products, arithmetic and copies ran while one was open for 0% of the time, Pallas kernels for 12%

profile of v5, /device:TPU:0, one launch (start us, length us, event | category | flops | bytes accessed | tf_op | source)
XLA Modules:
  0.0 17.6 jit_solution(12306778143404647304)
XLA Ops:
  0.0 0.0 copy-start
  0.7 0.1 table.1.table_ref
  0.8 0.4 %copy-done = f32[512,2,256]{2,1,0:T(2,128)S(1)} copy-done((f32[512,2,256]{2,1,0:T(2,128)S(1)}, f32[512,2,256]{2,1,0:T(2,128)}, u32[]{:S(2)}) %copy-start) | copy-done | bytes 1048600
  1.2 0.3 %transform.1 = (f32[32,128]{1,0:T(8,128)S(1)}, f32[32,128]{1,0:T(8,128)S(1)}) custom-call(bf16[64,512]{1,0:T(8,128)(2,1)S(1)} %table.1.table_ref, f32[2048,128]{1,0:T(8,128)S(1)} %bitcast.9), custom_call_target="tpu_custom_call" | custom-call | tf_op jit(solution)/shard_map/transform/pallas_call | solution.py:245
  1.6 0.0 copy-start.1
  1.6 0.0 copy-start.2
  1.6 0.6 %collective-permute-start.2 = (f32[32,128]{1,0:T(8,128)S(1)}, f32[32,128]{1,0:T(8,128)S(1)}, u32[]{:S(2)}, u32[]{:S(2)}) collective-permute-start(f32[32,128]{1,0:T(8,128)S(1)} %get-tuple-element.8), channel_id=1, source_target_pairs={{0,1},{1,0},{2,3},{3,2},{4,5},{5,4},{6,7},{7,6},{8,9},{9,8},{10,11... | collective-permute-start | bytes 49160 | tf_op jit(solution)/shard_map/ppermute | solution.py:216
  2.2 0.1 copy-done.1
  2.3 0.5 %collective-permute-start.1 = (s32[64,2]{0,1:T(2,128)S(1)}, s32[64,2]{0,1:T(2,128)S(1)}, u32[]{:S(2)}, u32[]{:S(2)}) collective-permute-start(s32[64,2]{0,1:T(2,128)S(1)} %copy-done.1), channel_id=1, source_target_pairs={{0,1},{1,0},{2,3},{3,2},{4,5},{5,4},{6,7},{7,6},{8,9},{9,8},{10,11... | collective-permute-start | bytes 1544 | tf_op jit(solution)/shard_map/ppermute | solution.py:216
  2.8 0.0 copy-done.2
  2.8 0.0 collective-permute-start
  2.8 1.1 %collective-permute-done = s32[64]{0:T(128)S(1)} collective-permute-done((s32[64]{0:T(128)S(1)}, s32[64]{0:T(128)S(1)}, u32[]{:S(2)}, u32[]{:S(2)}) %collective-permute-start) | collective-permute-done | bytes 288 | tf_op jit(solution)/shard_map/ppermute | solution.py:216
  3.9 0.0 collective-permute-done.1
  3.9 0.8 %pack.1 = f32[8,128]{1,0:T(8,128)S(1)} custom-call(f32[32,128]{1,0:T(8,128)S(1)} %get-tuple-element.7.after_ref, s32[1,64]{1,0:T(1,128)} %bitcast.13, s32[2,64]{1,0:T(2,128)} %bitcast.12, s32[1,64]{1,0:T(1,128)S(1)} %bitcast.11, s32[2,64]{1,0:T(2,128)S(1)} %bitcast.10), custom_call_target="tpu_custom_call" | custom-call | tf_op jit(solution)/shard_map/pack/pallas_call | solution.py:253
  4.7 0.0 collective-permute-done.2
  4.8 2.7 %collective-permute-start.3 = (f32[24,128]{1,0:T(8,128)S(1)}, f32[24,128]{1,0:T(8,128)S(1)}, u32[]{:S(2)}, u32[]{:S(2)}) collective-permute-start(f32[24,128]{1,0:T(8,128)S(1)} %pad_maximum_fusion.after_ref), channel_id=1, source_target_pairs={{0,3},{1,2},{2,1},{3,0},{4,7},{5,6},{6,5},{7,4},{8,11},{9,10},{10,... | collective-permute-start | bytes 36872 | tf_op jit(solution)/shard_map/ppermute | solution.py:216
  7.5 1.4 %collective-permute-done.3 = f32[24,128]{1,0:T(8,128)S(1)} collective-permute-done((f32[24,128]{1,0:T(8,128)S(1)}, f32[24,128]{1,0:T(8,128)S(1)}, u32[]{:S(2)}, u32[]{:S(2)}) %collective-permute-start.3) | collective-permute-done | bytes 12320 | tf_op jit(solution)/shard_map/ppermute | solution.py:216
  8.9 1.8 %collective-permute-start.4 = (f32[16,128]{1,0:T(8,128)S(1)}, f32[16,128]{1,0:T(8,128)S(1)}, u32[]{:S(2)}, u32[]{:S(2)}) collective-permute-start(f32[16,128]{1,0:T(8,128)S(1)} %pad_maximum_fusion.2), channel_id=1, source_target_pairs={{0,5},{1,4},{2,7},{3,6},{4,1},{5,0},{6,3},{7,2},{8,13},{9,12},{10,... | collective-permute-start | bytes 24584 | tf_op jit(solution)/shard_map/ppermute | solution.py:216
  10.7 1.2 %fetch.1.transfer_ref = bf16[1,2,256,1024]{3,2,1,0:T(8,128)(2,1)S(1)} custom-call(f32[24,128]{1,0:T(8,128)S(1)} %pad_maximum_fusion.after_ref, bf16[1,2,256,1024]{3,2,1,0:T(8,128)(2,1)} %transfer_hbm.1), custom_call_target="tpu_custom_call" | custom-call | tf_op jit(solution)/shard_map/fetch/pallas_call | solution.py:277
  12.0 0.1 collective-permute-done.4
  12.1 2.8 %collective-permute-start.5 = (f32[20,128]{1,0:T(8,128)S(1)}, f32[20,128]{1,0:T(8,128)S(1)}, u32[]{:S(2)}, u32[]{:S(2)}) collective-permute-start(f32[20,128]{1,0:T(8,128)S(1)} %pad_maximum_fusion.1), channel_id=1, source_target_pairs={{0,9},{1,8},{2,11},{3,10},{4,13},{5,12},{6,15},{7,14},{8,1},{9,0},... | collective-permute-start | bytes 30728 | tf_op jit(solution)/shard_map/ppermute | solution.py:216
  14.9 0.2 count.1.count_ref
  15.1 1.2 %collective-permute-done.5.got_ref = f32[20,128]{1,0:T(8,128)S(1)} collective-permute-done((f32[20,128]{1,0:T(8,128)S(1)}, f32[20,128]{1,0:T(8,128)S(1)}, u32[]{:S(2)}, u32[]{:S(2)}) %collective-permute-start.5) | collective-permute-done | bytes 10272 | tf_op jit(solution)/shard_map/ppermute | solution.py:216
  16.3 1.3 %residual.1 = f32[1,2,1024]{2,1,0:T(2,128)} custom-call(f32[1,32,128]{2,1,0:T(8,128)S(1)} %count.1.count_ref, f32[4,128]{1,0:T(4,128)S(1)} %get-tuple-element.12.held_ref, f32[20,128]{1,0:T(8,128)S(1)} %collective-permute-done.5.got_ref, bf16[1,2,256,1024]{3,2,1,0:T(8,128)(2,1)S(1)} %fetch.1.transfer_ref), custom_call_target="tpu_custom_call" | custom-call | tf_op jit(solution)/shard_map/residual/pallas_call | solution.py:295
  (11 shorter events, 0.0 us)
Async XLA Ops:
  0.0 1.2 %copy-start = (f32[512,2,256]{2,1,0:T(2,128)S(1)}, f32[512,2,256]{2,1,0:T(2,128)}, u32[]{:S(2)}) copy-start(f32[512,2,256]{2,1,0:T(2,128)} %param.5) | copy-start | bytes 3145732
  1.6 0.7 %copy-start.1 = (s32[64,2]{0,1:T(2,128)S(1)}, s32[64,2]{0,1:T(2,128)}, u32[]{:S(2)}) copy-start(s32[64,2]{0,1:T(2,128)} %param.9) | copy-start | bytes 1540
  1.6 1.2 %copy-start.2 = (s32[64]{0:T(128)S(1)}, s32[64]{0:T(128)}, u32[]{:S(2)}) copy-start(s32[64]{0:T(128)} %param.8) | copy-start | bytes 772
  1.6 3.1 %collective-permute-start.2 = (f32[32,128]{1,0:T(8,128)S(1)}, f32[32,128]{1,0:T(8,128)S(1)}, u32[]{:S(2)}, u32[]{:S(2)}) collective-permute-start(f32[32,128]{1,0:T(8,128)S(1)} %get-tuple-element.8), channel_id=1, source_target_pairs={{0,1},{1,0},{2,3},{3,2},{4,5},{5,4},{6,7},{7,6},{8,9},{9,8},{10,11... | collective-permute-start | bytes 49160 | tf_op jit(solution)/shard_map/ppermute | solution.py:216
  2.3 1.7 %collective-permute-start.1 = (s32[64,2]{0,1:T(2,128)S(1)}, s32[64,2]{0,1:T(2,128)S(1)}, u32[]{:S(2)}, u32[]{:S(2)}) collective-permute-start(s32[64,2]{0,1:T(2,128)S(1)} %copy-done.1), channel_id=1, source_target_pairs={{0,1},{1,0},{2,3},{3,2},{4,5},{5,4},{6,7},{7,6},{8,9},{9,8},{10,11... | collective-permute-start | bytes 1544 | tf_op jit(solution)/shard_map/ppermute | solution.py:216
  2.8 1.2 %collective-permute-start = (s32[64]{0:T(128)S(1)}, s32[64]{0:T(128)S(1)}, u32[]{:S(2)}, u32[]{:S(2)}) collective-permute-start(s32[64]{0:T(128)S(1)} %copy-done.2), channel_id=1, source_target_pairs={{0,1},{1,0},{2,3},{3,2},{4,5},{5,4},{6,7},{7,6},{8,9},{9,8},{10,11... | collective-permute-start | bytes 776 | tf_op jit(solution)/shard_map/ppermute | solution.py:216
  4.8 4.1 %collective-permute-start.3 = (f32[24,128]{1,0:T(8,128)S(1)}, f32[24,128]{1,0:T(8,128)S(1)}, u32[]{:S(2)}, u32[]{:S(2)}) collective-permute-start(f32[24,128]{1,0:T(8,128)S(1)} %pad_maximum_fusion.after_ref), channel_id=1, source_target_pairs={{0,3},{1,2},{2,1},{3,0},{4,7},{5,6},{6,5},{7,4},{8,11},{9,10},{10,... | collective-permute-start | bytes 36872 | tf_op jit(solution)/shard_map/ppermute | solution.py:216
  8.9 3.2 %collective-permute-start.4 = (f32[16,128]{1,0:T(8,128)S(1)}, f32[16,128]{1,0:T(8,128)S(1)}, u32[]{:S(2)}, u32[]{:S(2)}) collective-permute-start(f32[16,128]{1,0:T(8,128)S(1)} %pad_maximum_fusion.2), channel_id=1, source_target_pairs={{0,5},{1,4},{2,7},{3,6},{4,1},{5,0},{6,3},{7,2},{8,13},{9,12},{10,... | collective-permute-start | bytes 24584 | tf_op jit(solution)/shard_map/ppermute | solution.py:216
  12.1 4.2 %collective-permute-start.5 = (f32[20,128]{1,0:T(8,128)S(1)}, f32[20,128]{1,0:T(8,128)S(1)}, u32[]{:S(2)}, u32[]{:S(2)}) collective-permute-start(f32[20,128]{1,0:T(8,128)S(1)} %pad_maximum_fusion.1), channel_id=1, source_target_pairs={{0,9},{1,8},{2,11},{3,10},{4,13},{5,12},{6,15},{7,14},{8,1},{9,0},... | collective-permute-start | bytes 30728 | tf_op jit(solution)/shard_map/ppermute | solution.py:216

commit v6 on v5

--- a/solution.py
+++ b/solution.py
@@ -165,7 +165,7 @@
         count_ref[local] = counts_of(held_ref[...], comps, base, groups)
 
 
-def residual_kernel(m_local, pieces, comps, count_ref, held_ref, got_ref, transfer_ref, out_ref):
+def residual_kernel(m_local, pieces, comps, count_ref, held_ref, got_ref, transfer_ref, turned_ref, out_ref):
     width = transfer_ref.shape[3]
     tiles = pieces // 2
     groups = width // LANES
@@ -184,8 +184,8 @@
         model_alm = jnp.concatenate(model, 0).astype(jnp.bfloat16)
 
         real_matrix, imag_matrix = transfer_ref[local, 0], transfer_ref[local, 1]
-        by_real = lax.dot_general(model_alm, real_matrix, NT, preferred_element_type=jnp.float32)
-        by_imag = lax.dot_general(model_alm, imag_matrix, NT, preferred_element_type=jnp.float32)
+        predicted = jnp.dot(model_alm, turned_ref[local], preferred_element_type=jnp.float32)
+        by_real, by_imag = predicted[:, : tiles * LANES], predicted[:, tiles * LANES :]
         pred_real = by_real[0:1] - by_imag[1:2]
         pred_imag = by_real[1:2] + by_imag[0:1]
         start = local * pieces
@@ -202,6 +202,13 @@
             out_ref[local, :, block] = jnp.dot(
                 with_real, real_matrix[:, block], preferred_element_type=jnp.float32
             ) + jnp.dot(with_imag, imag_matrix[:, block], preferred_element_type=jnp.float32)
+
+
+def turn_kernel(after_ref, transfer_ref, turned_ref):
+    m_local, _, baselines, _ = transfer_ref.shape
+    for local in range(m_local):
+        for part in range(2):
+            turned_ref[local, :, part * baselines : (part + 1) * baselines] = transfer_ref[local, part].T
 
 
 def in_hbm(value):
@@ -292,14 +299,22 @@
         compiler_params=params,
         name="count",
     )(in_vmem(components))
+    turned = pl.pallas_call(
+        turn_kernel,
+        out_shape=pltpu.VMEM((m_local, width, 2 * baselines), transfer.dtype),
+        in_specs=[vmem, vmem],
+        out_specs=vmem,
+        compiler_params=params,
+        name="turn",
+    )(in_vmem(components), in_vmem(matrices))
     return pl.pallas_call(
         functools.partial(residual_kernel, m_local, pieces, comps),
         out_shape=jax.ShapeDtypeStruct((m_local, 2, width), jnp.float32),
-        in_specs=[vmem, vmem, vmem, vmem],
+        in_specs=[vmem] * 5,
         out_specs=vmem,
         compiler_params=params,
         name="residual",
-    )(in_vmem(count), in_vmem(spectra), in_vmem(got), in_vmem(matrices))
+    )(in_vmem(count), in_vmem(spectra), in_vmem(got), in_vmem(matrices), in_vmem(turned))
 
 
 def solution(mesh):

time: 17.8 us -> 17.7 us (level)
  waiting for transfers between devices: 3.93 us -> 3.59 us
  Pallas kernels: 3.86 us -> 4.1 us
    ppermute x6, waiting for transfers between devices: 3.93 us -> 3.59 us  [swap(): lax.ppermute(value, 'ma', [(device, device ^ offset) for device in range(...]
    pallas_call x0 -> x1, Pallas kernels: none -> 0.34 us  [body(): pl.pallas_call(turn_kernel, out_shape=pltpu.VMEM((m_local, width, 2 * bas...]
  transfers between devices with their start and end apart: 6 -> 6, of which waited for: 4 -> 4; matrix products, arithmetic and copies ran while one was open for 0% -> 0% of each run, Pallas kernels for 12% -> 14%
where the time goes in v6:
time: 17.7 us; the launch traced here: 17.5 us
  starting transfers between devices  8.37 us (47%)
  Pallas kernels  4.1 us (23%)
  waiting for transfers between devices  3.59 us (20%)
  between operations  0.83 us (5%)
  local copies, waits for them, and re-layouts  0.59 us (3%)
    ppermute x6, starting transfers between devices, swap(): lax.ppermute(value, 'ma', [(device, device ^ offset) for device in range(...  8.37 us
    ppermute x6, waiting for transfers between devices, swap(): lax.ppermute(value, 'ma', [(device, device ^ offset) for device in range(...  3.59 us
    pallas_call x1, Pallas kernels, body(): pl.pallas_call(fetch_kernel, out_shape=pltpu.VMEM(transfer.shape, transfe...  1.23 us
    pallas_call x1, Pallas kernels, body(): pl.pallas_call(functools.partial(residual_kernel, m_local, pieces, comps)...  1.21 us
    pallas_call x1, Pallas kernels, body(): pl.pallas_call(pack_kernel, out_shape=pltpu.VMEM((unit, LANES), jnp.float...  0.79 us
    unnamed x6, local copies, waits for them, and re-layouts  0.57 us
  transfers between devices with their start and end apart: 6, of which 4 were waited for; matrix products, arithmetic and copies ran while one was open for 0% of the time, Pallas kernels for 14%

profile of v6, /device:TPU:0, one launch (start us, length us, event | category | flops | bytes accessed | tf_op | source)
XLA Modules:
  0.0 17.5 jit_solution(7602225178578265926)
XLA Ops:
  0.0 0.0 copy-start
  0.7 0.1 table.1.table_ref
  0.8 0.4 %copy-done = f32[512,2,256]{2,1,0:T(2,128)S(1)} copy-done((f32[512,2,256]{2,1,0:T(2,128)S(1)}, f32[512,2,256]{2,1,0:T(2,128)}, u32[]{:S(2)}) %copy-start) | copy-done | bytes 1048600
  1.2 0.3 %transform.1 = (f32[32,128]{1,0:T(8,128)S(1)}, f32[32,128]{1,0:T(8,128)S(1)}) custom-call(bf16[64,512]{1,0:T(8,128)(2,1)S(1)} %table.1.table_ref, f32[2048,128]{1,0:T(8,128)S(1)} %bitcast.9), custom_call_target="tpu_custom_call" | custom-call | tf_op jit(solution)/shard_map/transform/pallas_call | solution.py:252
  1.6 0.0 copy-start.1
  1.6 0.0 copy-start.2
  1.6 0.6 %collective-permute-start.2 = (f32[32,128]{1,0:T(8,128)S(1)}, f32[32,128]{1,0:T(8,128)S(1)}, u32[]{:S(2)}, u32[]{:S(2)}) collective-permute-start(f32[32,128]{1,0:T(8,128)S(1)} %get-tuple-element.8), channel_id=1, source_target_pairs={{0,1},{1,0},{2,3},{3,2},{4,5},{5,4},{6,7},{7,6},{8,9},{9,8},{10,11... | collective-permute-start | bytes 49160 | tf_op jit(solution)/shard_map/ppermute | solution.py:223
  2.2 0.1 copy-done.1
  2.3 0.5 %collective-permute-start.1 = (s32[64,2]{0,1:T(2,128)S(1)}, s32[64,2]{0,1:T(2,128)S(1)}, u32[]{:S(2)}, u32[]{:S(2)}) collective-permute-start(s32[64,2]{0,1:T(2,128)S(1)} %copy-done.1), channel_id=1, source_target_pairs={{0,1},{1,0},{2,3},{3,2},{4,5},{5,4},{6,7},{7,6},{8,9},{9,8},{10,11... | collective-permute-start | bytes 1544 | tf_op jit(solution)/shard_map/ppermute | solution.py:223
  2.8 0.0 copy-done.2
  2.8 0.0 collective-permute-start
  2.8 1.1 %collective-permute-done = s32[64]{0:T(128)S(1)} collective-permute-done((s32[64]{0:T(128)S(1)}, s32[64]{0:T(128)S(1)}, u32[]{:S(2)}, u32[]{:S(2)}) %collective-permute-start) | collective-permute-done | bytes 288 | tf_op jit(solution)/shard_map/ppermute | solution.py:223
  3.9 0.0 collective-permute-done.1
  3.9 0.8 %pack.1 = f32[8,128]{1,0:T(8,128)S(1)} custom-call(f32[32,128]{1,0:T(8,128)S(1)} %get-tuple-element.7.after_ref, s32[1,64]{1,0:T(1,128)} %bitcast.13, s32[2,64]{1,0:T(2,128)} %bitcast.12, s32[1,64]{1,0:T(1,128)S(1)} %bitcast.11, s32[2,64]{1,0:T(2,128)S(1)} %bitcast.10), custom_call_target="tpu_custom_call" | custom-call | tf_op jit(solution)/shard_map/pack/pallas_call | solution.py:260
  4.7 0.0 collective-permute-done.2
  4.8 2.7 %collective-permute-start.3 = (f32[24,128]{1,0:T(8,128)S(1)}, f32[24,128]{1,0:T(8,128)S(1)}, u32[]{:S(2)}, u32[]{:S(2)}) collective-permute-start(f32[24,128]{1,0:T(8,128)S(1)} %pad_maximum_fusion.after_ref), channel_id=1, source_target_pairs={{0,3},{1,2},{2,1},{3,0},{4,7},{5,6},{6,5},{7,4},{8,11},{9,10},{10,... | collective-permute-start | bytes 36872 | tf_op jit(solution)/shard_map/ppermute | solution.py:223
  7.5 1.4 %collective-permute-done.3 = f32[24,128]{1,0:T(8,128)S(1)} collective-permute-done((f32[24,128]{1,0:T(8,128)S(1)}, f32[24,128]{1,0:T(8,128)S(1)}, u32[]{:S(2)}, u32[]{:S(2)}) %collective-permute-start.3) | collective-permute-done | bytes 12320 | tf_op jit(solution)/shard_map/ppermute | solution.py:223
  8.9 1.8 %collective-permute-start.4 = (f32[16,128]{1,0:T(8,128)S(1)}, f32[16,128]{1,0:T(8,128)S(1)}, u32[]{:S(2)}, u32[]{:S(2)}) collective-permute-start(f32[16,128]{1,0:T(8,128)S(1)} %pad_maximum_fusion.2), channel_id=1, source_target_pairs={{0,5},{1,4},{2,7},{3,6},{4,1},{5,0},{6,3},{7,2},{8,13},{9,12},{10,... | collective-permute-start | bytes 24584 | tf_op jit(solution)/shard_map/ppermute | solution.py:223
  10.7 1.2 %fetch.1.transfer_ref = bf16[1,2,256,1024]{3,2,1,0:T(8,128)(2,1)S(1)} custom-call(f32[24,128]{1,0:T(8,128)S(1)} %pad_maximum_fusion.after_ref, bf16[1,2,256,1024]{3,2,1,0:T(8,128)(2,1)} %transfer_hbm.1), custom_call_target="tpu_custom_call" | custom-call | tf_op jit(solution)/shard_map/fetch/pallas_call | solution.py:284
  12.0 0.1 collective-permute-done.4
  12.1 2.8 %collective-permute-start.5 = (f32[20,128]{1,0:T(8,128)S(1)}, f32[20,128]{1,0:T(8,128)S(1)}, u32[]{:S(2)}, u32[]{:S(2)}) collective-permute-start(f32[20,128]{1,0:T(8,128)S(1)} %pad_maximum_fusion.1), channel_id=1, source_target_pairs={{0,9},{1,8},{2,11},{3,10},{4,13},{5,12},{6,15},{7,14},{8,1},{9,0},... | collective-permute-start | bytes 30728 | tf_op jit(solution)/shard_map/ppermute | solution.py:223
  14.9 0.2 count.1.count_ref
  15.1 0.3 %turn.1.turned_ref = bf16[1,1024,512]{2,1,0:T(8,128)(2,1)S(1)} custom-call(f32[16,128]{1,0:T(8,128)S(1)} %pad_maximum_fusion.3.held_ref.after_ref, bf16[1,2,256,1024]{3,2,1,0:T(8,128)(2,1)S(1)} %fetch.1.transfer_ref), custom_call_target="tpu_custom_call" | custom-call | tf_op jit(solution)/shard_map/turn/pallas_call | solution.py:302
  15.4 0.9 %collective-permute-done.5.got_ref = f32[20,128]{1,0:T(8,128)S(1)} collective-permute-done((f32[20,128]{1,0:T(8,128)S(1)}, f32[20,128]{1,0:T(8,128)S(1)}, u32[]{:S(2)}, u32[]{:S(2)}) %collective-permute-start.5) | collective-permute-done | bytes 10272 | tf_op jit(solution)/shard_map/ppermute | solution.py:223
  16.3 1.2 %residual.1 = f32[1,2,1024]{2,1,0:T(2,128)} custom-call(f32[1,32,128]{2,1,0:T(8,128)S(1)} %count.1.count_ref, f32[4,128]{1,0:T(4,128)S(1)} %get-tuple-element.12.held_ref, f32[20,128]{1,0:T(8,128)S(1)} %collective-permute-done.5.got_ref, bf16[1,2,256,1024]{3,2,1,0:T(8,128)(2,1)S(1)} %fetch.1.transfer_ref, bf16[1,1024,512]{2,1,0:T(8,128)(2,1)S(1)} %turn.1.turned_ref), custom_call_target="tpu_custom_call" | custom-call | tf_op jit(solution)/shard_map/residual/pallas_call | solution.py:310
  (11 shorter events, 0.0 us)
Async XLA Ops:
  0.0 1.2 %copy-start = (f32[512,2,256]{2,1,0:T(2,128)S(1)}, f32[512,2,256]{2,1,0:T(2,128)}, u32[]{:S(2)}) copy-start(f32[512,2,256]{2,1,0:T(2,128)} %param.5) | copy-start | bytes 3145732
  1.6 0.7 %copy-start.1 = (s32[64,2]{0,1:T(2,128)S(1)}, s32[64,2]{0,1:T(2,128)}, u32[]{:S(2)}) copy-start(s32[64,2]{0,1:T(2,128)} %param.9) | copy-start | bytes 1540
  1.6 1.2 %copy-start.2 = (s32[64]{0:T(128)S(1)}, s32[64]{0:T(128)}, u32[]{:S(2)}) copy-start(s32[64]{0:T(128)} %param.8) | copy-start | bytes 772
  1.6 3.1 %collective-permute-start.2 = (f32[32,128]{1,0:T(8,128)S(1)}, f32[32,128]{1,0:T(8,128)S(1)}, u32[]{:S(2)}, u32[]{:S(2)}) collective-permute-start(f32[32,128]{1,0:T(8,128)S(1)} %get-tuple-element.8), channel_id=1, source_target_pairs={{0,1},{1,0},{2,3},{3,2},{4,5},{5,4},{6,7},{7,6},{8,9},{9,8},{10,11... | collective-permute-start | bytes 49160 | tf_op jit(solution)/shard_map/ppermute | solution.py:223
  2.3 1.7 %collective-permute-start.1 = (s32[64,2]{0,1:T(2,128)S(1)}, s32[64,2]{0,1:T(2,128)S(1)}, u32[]{:S(2)}, u32[]{:S(2)}) collective-permute-start(s32[64,2]{0,1:T(2,128)S(1)} %copy-done.1), channel_id=1, source_target_pairs={{0,1},{1,0},{2,3},{3,2},{4,5},{5,4},{6,7},{7,6},{8,9},{9,8},{10,11... | collective-permute-start | bytes 1544 | tf_op jit(solution)/shard_map/ppermute | solution.py:223
  2.8 1.2 %collective-permute-start = (s32[64]{0:T(128)S(1)}, s32[64]{0:T(128)S(1)}, u32[]{:S(2)}, u32[]{:S(2)}) collective-permute-start(s32[64]{0:T(128)S(1)} %copy-done.2), channel_id=1, source_target_pairs={{0,1},{1,0},{2,3},{3,2},{4,5},{5,4},{6,7},{7,6},{8,9},{9,8},{10,11... | collective-permute-start | bytes 776 | tf_op jit(solution)/shard_map/ppermute | solution.py:223
  4.8 4.1 %collective-permute-start.3 = (f32[24,128]{1,0:T(8,128)S(1)}, f32[24,128]{1,0:T(8,128)S(1)}, u32[]{:S(2)}, u32[]{:S(2)}) collective-permute-start(f32[24,128]{1,0:T(8,128)S(1)} %pad_maximum_fusion.after_ref), channel_id=1, source_target_pairs={{0,3},{1,2},{2,1},{3,0},{4,7},{5,6},{6,5},{7,4},{8,11},{9,10},{10,... | collective-permute-start | bytes 36872 | tf_op jit(solution)/shard_map/ppermute | solution.py:223
  8.9 3.2 %collective-permute-start.4 = (f32[16,128]{1,0:T(8,128)S(1)}, f32[16,128]{1,0:T(8,128)S(1)}, u32[]{:S(2)}, u32[]{:S(2)}) collective-permute-start(f32[16,128]{1,0:T(8,128)S(1)} %pad_maximum_fusion.2), channel_id=1, source_target_pairs={{0,5},{1,4},{2,7},{3,6},{4,1},{5,0},{6,3},{7,2},{8,13},{9,12},{10,... | collective-permute-start | bytes 24584 | tf_op jit(solution)/shard_map/ppermute | solution.py:223
  12.1 4.2 %collective-permute-start.5 = (f32[20,128]{1,0:T(8,128)S(1)}, f32[20,128]{1,0:T(8,128)S(1)}, u32[]{:S(2)}, u32[]{:S(2)}) collective-permute-start(f32[20,128]{1,0:T(8,128)S(1)} %pad_maximum_fusion.1), channel_id=1, source_target_pairs={{0,9},{1,8},{2,11},{3,10},{4,13},{5,12},{6,15},{7,14},{8,1},{9,0},... | collective-permute-start | bytes 30728 | tf_op jit(solution)/shard_map/ppermute | solution.py:223

commit v7 on v6

--- a/solution.py
+++ b/solution.py
@@ -112,12 +112,18 @@
     tiles = pieces // 2
     half, size = devices // 2, m_local * pieces
     scale = 1.0 / math.sqrt(ticks)
+    steps = 4 if samples % 64 == 0 else 1
+    depth = samples // steps
     for tile in range(tiles):
-        parts = [vis_ref[pl.ds(tile * 2 + part, samples, stride=pieces), :] for part in range(2)]
-        high, low = halves(jnp.concatenate(parts, 1))
-        product = jnp.dot(table_ref[...], high, preferred_element_type=jnp.float32)
-        product += jnp.dot(table_ref[...], low, preferred_element_type=jnp.float32)
-        product = product[: 2 * modes] + product[2 * modes :]
+        product, smaller = 0.0, 0.0
+        for step in range(steps):
+            first = step * depth
+            parts = [vis_ref[pl.ds(first * pieces + tile * 2 + part, depth, stride=pieces), :] for part in range(2)]
+            high, low = halves(jnp.concatenate(parts, 1))
+            columns = slice(first, first + depth)
+            product += jnp.dot(table_ref[:, columns], high, preferred_element_type=jnp.float32)
+            smaller += jnp.dot(table_ref[: 2 * modes, columns], low, preferred_element_type=jnp.float32)
+        product = product[: 2 * modes] + (product[2 * modes :] + smaller)
         from_cos, from_sin = product[:modes], product[modes:]
         real_part = (from_cos[:, :LANES] + from_sin[:, LANES:]) * scale
         imag_part = (from_cos[:, LANES:] - from_sin[:, :LANES]) * scale

time: 17.7 us -> 17.7 us (level)
  no operation moved by 1% of the time
where the time goes in v7:
time: 17.7 us; the launch traced here: 17.5 us
  starting transfers between devices  8.37 us (47%)
  Pallas kernels  4.08 us (23%)
  waiting for transfers between devices  3.59 us (20%)
  between operations  0.83 us (5%)
  local copies, waits for them, and re-layouts  0.57 us (3%)
    ppermute x6, starting transfers between devices, swap(): lax.ppermute(value, 'ma', [(device, device ^ offset) for device in range(...  8.37 us
    ppermute x6, waiting for transfers between devices, swap(): lax.ppermute(value, 'ma', [(device, device ^ offset) for device in range(...  3.59 us
    pallas_call x1, Pallas kernels, body(): pl.pallas_call(fetch_kernel, out_shape=pltpu.VMEM(transfer.shape, transfe...  1.23 us
    pallas_call x1, Pallas kernels, body(): pl.pallas_call(functools.partial(residual_kernel, m_local, pieces, comps)...  1.21 us
    pallas_call x1, Pallas kernels, body(): pl.pallas_call(pack_kernel, out_shape=pltpu.VMEM((unit, LANES), jnp.float...  0.79 us
    unnamed x6, local copies, waits for them, and re-layouts  0.56 us
  transfers between devices with their start and end apart: 6, of which 4 were waited for; matrix products, arithmetic and copies ran while one was open for 0% of the time, Pallas kernels for 14%

profile of v7, /device:TPU:0, one launch (start us, length us, event | category | flops | bytes accessed | tf_op | source)
XLA Modules:
  0.0 17.5 jit_solution(17330264692400524661)
XLA Ops:
  0.0 0.0 copy-start
  0.7 0.1 table.1.table_ref
  0.8 0.4 %copy-done = f32[512,2,256]{2,1,0:T(2,128)S(1)} copy-done((f32[512,2,256]{2,1,0:T(2,128)S(1)}, f32[512,2,256]{2,1,0:T(2,128)}, u32[]{:S(2)}) %copy-start) | copy-done | bytes 1048600
  1.2 0.3 %transform.1 = (f32[32,128]{1,0:T(8,128)S(1)}, f32[32,128]{1,0:T(8,128)S(1)}) custom-call(bf16[64,512]{1,0:T(8,128)(2,1)S(1)} %table.1.table_ref, f32[2048,128]{1,0:T(8,128)S(1)} %bitcast.9), custom_call_target="tpu_custom_call" | custom-call | tf_op jit(solution)/shard_map/transform/pallas_call | solution.py:258
  1.5 0.0 copy-start.1
  1.5 0.0 copy-start.2
  1.6 0.6 %collective-permute-start.2 = (f32[32,128]{1,0:T(8,128)S(1)}, f32[32,128]{1,0:T(8,128)S(1)}, u32[]{:S(2)}, u32[]{:S(2)}) collective-permute-start(f32[32,128]{1,0:T(8,128)S(1)} %get-tuple-element.8), channel_id=1, source_target_pairs={{0,1},{1,0},{2,3},{3,2},{4,5},{5,4},{6,7},{7,6},{8,9},{9,8},{10,11... | collective-permute-start | bytes 49160 | tf_op jit(solution)/shard_map/ppermute | solution.py:229
  2.1 0.1 copy-done.1
  2.2 0.5 %collective-permute-start.1 = (s32[64,2]{0,1:T(2,128)S(1)}, s32[64,2]{0,1:T(2,128)S(1)}, u32[]{:S(2)}, u32[]{:S(2)}) collective-permute-start(s32[64,2]{0,1:T(2,128)S(1)} %copy-done.1), channel_id=1, source_target_pairs={{0,1},{1,0},{2,3},{3,2},{4,5},{5,4},{6,7},{7,6},{8,9},{9,8},{10,11... | collective-permute-start | bytes 1544 | tf_op jit(solution)/shard_map/ppermute | solution.py:229
  2.7 0.0 copy-done.2
  2.7 0.0 collective-permute-start
  2.7 1.1 %collective-permute-done = s32[64]{0:T(128)S(1)} collective-permute-done((s32[64]{0:T(128)S(1)}, s32[64]{0:T(128)S(1)}, u32[]{:S(2)}, u32[]{:S(2)}) %collective-permute-start) | collective-permute-done | bytes 288 | tf_op jit(solution)/shard_map/ppermute | solution.py:229
  3.9 0.0 collective-permute-done.1
  3.9 0.8 %pack.1 = f32[8,128]{1,0:T(8,128)S(1)} custom-call(f32[32,128]{1,0:T(8,128)S(1)} %get-tuple-element.7.after_ref, s32[1,64]{1,0:T(1,128)} %bitcast.13, s32[2,64]{1,0:T(2,128)} %bitcast.12, s32[1,64]{1,0:T(1,128)S(1)} %bitcast.11, s32[2,64]{1,0:T(2,128)S(1)} %bitcast.10), custom_call_target="tpu_custom_call" | custom-call | tf_op jit(solution)/shard_map/pack/pallas_call | solution.py:266
  4.7 0.0 collective-permute-done.2
  4.7 2.7 %collective-permute-start.3 = (f32[24,128]{1,0:T(8,128)S(1)}, f32[24,128]{1,0:T(8,128)S(1)}, u32[]{:S(2)}, u32[]{:S(2)}) collective-permute-start(f32[24,128]{1,0:T(8,128)S(1)} %pad_maximum_fusion.after_ref), channel_id=1, source_target_pairs={{0,3},{1,2},{2,1},{3,0},{4,7},{5,6},{6,5},{7,4},{8,11},{9,10},{10,... | collective-permute-start | bytes 36872 | tf_op jit(solution)/shard_map/ppermute | solution.py:229
  7.4 1.4 %collective-permute-done.3 = f32[24,128]{1,0:T(8,128)S(1)} collective-permute-done((f32[24,128]{1,0:T(8,128)S(1)}, f32[24,128]{1,0:T(8,128)S(1)}, u32[]{:S(2)}, u32[]{:S(2)}) %collective-permute-start.3) | collective-permute-done | bytes 12320 | tf_op jit(solution)/shard_map/ppermute | solution.py:229
  8.8 1.8 %collective-permute-start.4 = (f32[16,128]{1,0:T(8,128)S(1)}, f32[16,128]{1,0:T(8,128)S(1)}, u32[]{:S(2)}, u32[]{:S(2)}) collective-permute-start(f32[16,128]{1,0:T(8,128)S(1)} %pad_maximum_fusion.2), channel_id=1, source_target_pairs={{0,5},{1,4},{2,7},{3,6},{4,1},{5,0},{6,3},{7,2},{8,13},{9,12},{10,... | collective-permute-start | bytes 24584 | tf_op jit(solution)/shard_map/ppermute | solution.py:229
  10.7 1.2 %fetch.1.transfer_ref = bf16[1,2,256,1024]{3,2,1,0:T(8,128)(2,1)S(1)} custom-call(f32[24,128]{1,0:T(8,128)S(1)} %pad_maximum_fusion.after_ref, bf16[1,2,256,1024]{3,2,1,0:T(8,128)(2,1)} %transfer_hbm.1), custom_call_target="tpu_custom_call" | custom-call | tf_op jit(solution)/shard_map/fetch/pallas_call | solution.py:290
  11.9 0.1 collective-permute-done.4
  12.1 2.8 %collective-permute-start.5 = (f32[20,128]{1,0:T(8,128)S(1)}, f32[20,128]{1,0:T(8,128)S(1)}, u32[]{:S(2)}, u32[]{:S(2)}) collective-permute-start(f32[20,128]{1,0:T(8,128)S(1)} %pad_maximum_fusion.1), channel_id=1, source_target_pairs={{0,9},{1,8},{2,11},{3,10},{4,13},{5,12},{6,15},{7,14},{8,1},{9,0},... | collective-permute-start | bytes 30728 | tf_op jit(solution)/shard_map/ppermute | solution.py:229
  14.9 0.2 count.1.count_ref
  15.0 0.3 %turn.1.turned_ref = bf16[1,1024,512]{2,1,0:T(8,128)(2,1)S(1)} custom-call(f32[16,128]{1,0:T(8,128)S(1)} %pad_maximum_fusion.3.held_ref.after_ref, bf16[1,2,256,1024]{3,2,1,0:T(8,128)(2,1)S(1)} %fetch.1.transfer_ref), custom_call_target="tpu_custom_call" | custom-call | tf_op jit(solution)/shard_map/turn/pallas_call | solution.py:308
  15.4 0.9 %collective-permute-done.5.got_ref = f32[20,128]{1,0:T(8,128)S(1)} collective-permute-done((f32[20,128]{1,0:T(8,128)S(1)}, f32[20,128]{1,0:T(8,128)S(1)}, u32[]{:S(2)}, u32[]{:S(2)}) %collective-permute-start.5) | collective-permute-done | bytes 10272 | tf_op jit(solution)/shard_map/ppermute | solution.py:229
  16.3 1.2 %residual.1 = f32[1,2,1024]{2,1,0:T(2,128)} custom-call(f32[1,32,128]{2,1,0:T(8,128)S(1)} %count.1.count_ref, f32[4,128]{1,0:T(4,128)S(1)} %get-tuple-element.12.held_ref, f32[20,128]{1,0:T(8,128)S(1)} %collective-permute-done.5.got_ref, bf16[1,2,256,1024]{3,2,1,0:T(8,128)(2,1)S(1)} %fetch.1.transfer_ref, bf16[1,1024,512]{2,1,0:T(8,128)(2,1)S(1)} %turn.1.turned_ref), custom_call_target="tpu_custom_call" | custom-call | tf_op jit(solution)/shard_map/residual/pallas_call | solution.py:316
  (11 shorter events, 0.0 us)
Async XLA Ops:
  0.0 1.2 %copy-start = (f32[512,2,256]{2,1,0:T(2,128)S(1)}, f32[512,2,256]{2,1,0:T(2,128)}, u32[]{:S(2)}) copy-start(f32[512,2,256]{2,1,0:T(2,128)} %param.5) | copy-start | bytes 3145732
  1.5 0.7 %copy-start.1 = (s32[64,2]{0,1:T(2,128)S(1)}, s32[64,2]{0,1:T(2,128)}, u32[]{:S(2)}) copy-start(s32[64,2]{0,1:T(2,128)} %param.9) | copy-start | bytes 1540
  1.5 1.2 %copy-start.2 = (s32[64]{0:T(128)S(1)}, s32[64]{0:T(128)}, u32[]{:S(2)}) copy-start(s32[64]{0:T(128)} %param.8) | copy-start | bytes 772
  1.6 3.1 %collective-permute-start.2 = (f32[32,128]{1,0:T(8,128)S(1)}, f32[32,128]{1,0:T(8,128)S(1)}, u32[]{:S(2)}, u32[]{:S(2)}) collective-permute-start(f32[32,128]{1,0:T(8,128)S(1)} %get-tuple-element.8), channel_id=1, source_target_pairs={{0,1},{1,0},{2,3},{3,2},{4,5},{5,4},{6,7},{7,6},{8,9},{9,8},{10,11... | collective-permute-start | bytes 49160 | tf_op jit(solution)/shard_map/ppermute | solution.py:229
  2.2 1.7 %collective-permute-start.1 = (s32[64,2]{0,1:T(2,128)S(1)}, s32[64,2]{0,1:T(2,128)S(1)}, u32[]{:S(2)}, u32[]{:S(2)}) collective-permute-start(s32[64,2]{0,1:T(2,128)S(1)} %copy-done.1), channel_id=1, source_target_pairs={{0,1},{1,0},{2,3},{3,2},{4,5},{5,4},{6,7},{7,6},{8,9},{9,8},{10,11... | collective-permute-start | bytes 1544 | tf_op jit(solution)/shard_map/ppermute | solution.py:229
  2.7 1.2 %collective-permute-start = (s32[64]{0:T(128)S(1)}, s32[64]{0:T(128)S(1)}, u32[]{:S(2)}, u32[]{:S(2)}) collective-permute-start(s32[64]{0:T(128)S(1)} %copy-done.2), channel_id=1, source_target_pairs={{0,1},{1,0},{2,3},{3,2},{4,5},{5,4},{6,7},{7,6},{8,9},{9,8},{10,11... | collective-permute-start | bytes 776 | tf_op jit(solution)/shard_map/ppermute | solution.py:229
  4.7 4.1 %collective-permute-start.3 = (f32[24,128]{1,0:T(8,128)S(1)}, f32[24,128]{1,0:T(8,128)S(1)}, u32[]{:S(2)}, u32[]{:S(2)}) collective-permute-start(f32[24,128]{1,0:T(8,128)S(1)} %pad_maximum_fusion.after_ref), channel_id=1, source_target_pairs={{0,3},{1,2},{2,1},{3,0},{4,7},{5,6},{6,5},{7,4},{8,11},{9,10},{10,... | collective-permute-start | bytes 36872 | tf_op jit(solution)/shard_map/ppermute | solution.py:229
  8.8 3.2 %collective-permute-start.4 = (f32[16,128]{1,0:T(8,128)S(1)}, f32[16,128]{1,0:T(8,128)S(1)}, u32[]{:S(2)}, u32[]{:S(2)}) collective-permute-start(f32[16,128]{1,0:T(8,128)S(1)} %pad_maximum_fusion.2), channel_id=1, source_target_pairs={{0,5},{1,4},{2,7},{3,6},{4,1},{5,0},{6,3},{7,2},{8,13},{9,12},{10,... | collective-permute-start | bytes 24584 | tf_op jit(solution)/shard_map/ppermute | solution.py:229
  12.1 4.2 %collective-permute-start.5 = (f32[20,128]{1,0:T(8,128)S(1)}, f32[20,128]{1,0:T(8,128)S(1)}, u32[]{:S(2)}, u32[]{:S(2)}) collective-permute-start(f32[20,128]{1,0:T(8,128)S(1)} %pad_maximum_fusion.1), channel_id=1, source_target_pairs={{0,9},{1,8},{2,11},{3,10},{4,13},{5,12},{6,15},{7,14},{8,1},{9,0},... | collective-permute-start | bytes 30728 | tf_op jit(solution)/shard_map/ppermute | solution.py:229

commit v8 on v7

--- a/solution.py
+++ b/solution.py
@@ -71,7 +71,7 @@
         table_ref[part * modes : (part + 1) * modes] = values[part % 2][part // 2]
 
 
-def pack_kernel(after_ref, index_hbm, amp_hbm, index_other_ref, amp_other_ref, tile_ref, index_ref, amp_ref, sems):
+def pack_kernel(kept_ref, index_hbm, amp_hbm, index_other_ref, amp_other_ref, tile_ref, index_ref, amp_ref, sems):
     copies = [
         pltpu.make_async_copy(index_hbm, index_ref, sems.at[0]),
         pltpu.make_async_copy(amp_hbm, amp_ref, sems.at[1]),
@@ -81,7 +81,9 @@
     comps = index_ref.shape[1]
     lanes, lines, _, _ = tile_of(comps)
     shared = LANES // lanes
-    tile_ref[...] = jnp.zeros(tile_ref.shape, jnp.float32)
+    unit = tile_of(comps)[3]
+    tile_ref[:unit] = jnp.zeros((unit, LANES), jnp.float32)
+    tile_ref[unit:] = kept_ref[...]
     for copy in copies:
         copy.wait()
     lane = lax.broadcasted_iota(jnp.int32, (1, LANES), 1) // lanes
@@ -111,6 +113,8 @@
     pieces = vis_ref.shape[0] // samples
     tiles = pieces // 2
     half, size = devices // 2, m_local * pieces
+    lead = send_ref.shape[0] - keep_ref.shape[0]
+    send_ref[:lead] = jnp.zeros((lead, LANES), jnp.float32)
     scale = 1.0 / math.sqrt(ticks)
     steps = 4 if samples % 64 == 0 else 1
     depth = samples // steps
@@ -131,7 +135,7 @@
             for part, value in enumerate((real_part, imag_part)):
                 start = local * pieces + part * tiles + tile
                 at = local * devices
-                send_ref[pl.ds(start, half, stride=size), :] = value[at : at + half]
+                send_ref[pl.ds(lead + start, half, stride=size), :] = value[at : at + half]
                 keep_ref[pl.ds(start, half, stride=size), :] = value[at + half : at + devices]
 
 
@@ -189,8 +193,13 @@
             model.append(jnp.concatenate([alm[g : g + 1] for g in range(groups)], 1))
         model_alm = jnp.concatenate(model, 0).astype(jnp.bfloat16)
 
-        real_matrix, imag_matrix = transfer_ref[local, 0], transfer_ref[local, 1]
-        predicted = jnp.dot(model_alm, turned_ref[local], preferred_element_type=jnp.float32)
+        predicted = jnp.concatenate(
+            [
+                jnp.dot(model_alm, turned_ref[local, :, at : at + BLOCK], preferred_element_type=jnp.float32)
+                for at in range(0, 2 * tiles * LANES, BLOCK)
+            ],
+            1,
+        )
         by_real, by_imag = predicted[:, : tiles * LANES], predicted[:, tiles * LANES :]
         pred_real = by_real[0:1] - by_imag[1:2]
         pred_imag = by_real[1:2] + by_imag[0:1]
@@ -201,13 +210,13 @@
         ]
         resid_real = (spectrum[0] - pred_real).astype(jnp.bfloat16)
         resid_imag = (spectrum[1] - pred_imag).astype(jnp.bfloat16)
-        with_real = jnp.concatenate([resid_real, resid_imag], 0)
-        with_imag = jnp.concatenate([resid_imag, -resid_real], 0)
+        both = jnp.concatenate(
+            [jnp.concatenate([resid_real, resid_imag], 1), jnp.concatenate([resid_imag, -resid_real], 1)], 0
+        )
+        matrix = transfer_ref[local].reshape(2 * tiles * LANES, width)
         for column in range(0, width, BLOCK):
             block = slice(column, column + BLOCK)
-            out_ref[local, :, block] = jnp.dot(
-                with_real, real_matrix[:, block], preferred_element_type=jnp.float32
-            ) + jnp.dot(with_imag, imag_matrix[:, block], preferred_element_type=jnp.float32)
+            out_ref[local, :, block] = jnp.dot(both, matrix[:, block], preferred_element_type=jnp.float32)
 
 
 def turn_kernel(after_ref, transfer_ref, turned_ref):
@@ -254,18 +263,19 @@
         cost_estimate=pl.CostEstimate(flops=LEAD, transcendentals=0, bytes_accessed=0),
         name="table",
     )(band_start)
-    part = pltpu.VMEM((devices // 2 * size, LANES), jnp.float32)
-    send, spectra = pl.pallas_call(
+    half_rows = devices // 2 * size
+    message = pltpu.VMEM((unit + half_rows, LANES), jnp.float32)
+    send, kept = pl.pallas_call(
         functools.partial(transform_kernel, samples * devices, m_local),
-        out_shape=(part, part),
+        out_shape=(message, pltpu.VMEM((half_rows, LANES), jnp.float32)),
         in_specs=[vmem, vmem],
         out_specs=(vmem, vmem),
         compiler_params=params,
         name="transform",
     )(in_vmem(table), in_vmem(lines))
-    components = pl.pallas_call(
+    held = pl.pallas_call(
         pack_kernel,
-        out_shape=pltpu.VMEM((unit, LANES), jnp.float32),
+        out_shape=message,
         in_specs=[vmem, hbm, hbm, vmem, vmem],
         out_specs=vmem,
         scratch_shapes=[
@@ -275,17 +285,19 @@
         ],
         compiler_params=params,
         name="pack",
-    )(in_vmem(spectra), in_hbm(index), in_hbm(amp), in_vmem(index_other), in_vmem(amp_other))
+    )(in_vmem(kept), in_hbm(index), in_hbm(amp), in_vmem(index_other), in_vmem(amp_other))
     got = swap(send, offsets[0], devices)
+    first = unit
     for step, offset in enumerate(offsets[1:], 1):
-        first = got.shape[0] - spectra.shape[0]
-        if step == 2:
-            components = components + got[:first]
-        elif step > 2:
-            components = jnp.concatenate([components, got[:first]], 0)
-        spectra = spectra + got[first:]
-        going = spectra.shape[0] // 2
-        send = jnp.concatenate([components, spectra[:going]], 0)
+        going = first + (held.shape[0] - first) // 2
+        if step <= 2:
+            send = held[:going] + got[:going]
+            held = jnp.concatenate([held[:first] + got[:first], held[going:] + got[going:]], 0)
+        else:
+            parcels = [held[:first], got[:first]]
+            send = jnp.concatenate(parcels + [held[first:going] + got[first:going]], 0)
+            held = jnp.concatenate(parcels + [held[going:] + got[going:]], 0)
+            first *= 2
         if step == 1:
             matrices = pl.pallas_call(
                 fetch_kernel,
@@ -296,7 +308,8 @@
                 compiler_params=params,
                 name="fetch",
             )(in_vmem(send), in_hbm(transfer))
-        got, spectra = swap(send, offset, devices), spectra[going:]
+        got = swap(send, offset, devices)
+    components, spectra = held[:first], held[first:]
     count = pl.pallas_call(
         functools.partial(count_kernel, m_local, width, comps),
         out_shape=pltpu.VMEM((m_local, 4 * width // LANES, LANES), jnp.float32),

time: 17.7 us -> 17.6 us (level)
  no operation moved by 1% of the time
where the time goes in v8:
time: 17.6 us; the launch traced here: 17.4 us
  starting transfers between devices  8.37 us (48%)
  Pallas kernels  4.08 us (23%)
  waiting for transfers between devices  3.58 us (20%)
  between operations  0.81 us (5%)
  local copies, waits for them, and re-layouts  0.56 us (3%)
    ppermute x6, starting transfers between devices, swap(): lax.ppermute(value, 'ma', [(device, device ^ offset) for device in range(...  8.37 us
    ppermute x6, waiting for transfers between devices, swap(): lax.ppermute(value, 'ma', [(device, device ^ offset) for device in range(...  3.58 us
    pallas_call x1, Pallas kernels, body(): pl.pallas_call(fetch_kernel, out_shape=pltpu.VMEM(transfer.shape, transfe...  1.23 us
    pallas_call x1, Pallas kernels, body(): pl.pallas_call(functools.partial(residual_kernel, m_local, pieces, comps)...  1.21 us
    pallas_call x1, Pallas kernels, body(): pl.pallas_call(pack_kernel, out_shape=message, in_specs=[vmem, hbm, hbm,...  0.79 us
    unnamed x6, local copies, waits for them, and re-layouts  0.56 us
  transfers between devices with their start and end apart: 6, of which 4 were waited for; matrix products, arithmetic and copies ran while one was open for 0% of the time, Pallas kernels for 14%

profile of v8, /device:TPU:0, one launch (start us, length us, event | category | flops | bytes accessed | tf_op | source)
XLA Modules:
  0.0 17.4 jit_solution(13743129101459671057)
XLA Ops:
  0.0 0.0 copy-start
  0.7 0.1 table.1.table_ref
  0.8 0.4 %copy-done = f32[512,2,256]{2,1,0:T(2,128)S(1)} copy-done((f32[512,2,256]{2,1,0:T(2,128)S(1)}, f32[512,2,256]{2,1,0:T(2,128)}, u32[]{:S(2)}) %copy-start) | copy-done | bytes 1048600
  1.2 0.3 %transform.1 = (f32[40,128]{1,0:T(8,128)S(1)}, f32[32,128]{1,0:T(8,128)S(1)}) custom-call(bf16[64,512]{1,0:T(8,128)(2,1)S(1)} %table.1.table_ref, f32[2048,128]{1,0:T(8,128)S(1)} %bitcast.9), custom_call_target="tpu_custom_call" | custom-call | tf_op jit(solution)/shard_map/transform/pallas_call | solution.py:268
  1.5 0.0 copy-start.1
  1.5 0.0 copy-start.2
  1.6 0.6 %collective-permute-start.2 = (f32[40,128]{1,0:T(8,128)S(1)}, f32[40,128]{1,0:T(8,128)S(1)}, u32[]{:S(2)}, u32[]{:S(2)}) collective-permute-start(f32[40,128]{1,0:T(8,128)S(1)} %get-tuple-element.8), channel_id=1, source_target_pairs={{0,1},{1,0},{2,3},{3,2},{4,5},{5,4},{6,7},{7,6},{8,9},{9,8},{10,11... | collective-permute-start | bytes 61448 | tf_op jit(solution)/shard_map/ppermute | solution.py:238
  2.1 0.1 copy-done.1
  2.2 0.5 %collective-permute-start.1 = (s32[64,2]{0,1:T(2,128)S(1)}, s32[64,2]{0,1:T(2,128)S(1)}, u32[]{:S(2)}, u32[]{:S(2)}) collective-permute-start(s32[64,2]{0,1:T(2,128)S(1)} %copy-done.1), channel_id=1, source_target_pairs={{0,1},{1,0},{2,3},{3,2},{4,5},{5,4},{6,7},{7,6},{8,9},{9,8},{10,11... | collective-permute-start | bytes 1544 | tf_op jit(solution)/shard_map/ppermute | solution.py:238
  2.7 0.0 copy-done.2
  2.7 0.0 collective-permute-start
  2.7 1.1 %collective-permute-done = s32[64]{0:T(128)S(1)} collective-permute-done((s32[64]{0:T(128)S(1)}, s32[64]{0:T(128)S(1)}, u32[]{:S(2)}, u32[]{:S(2)}) %collective-permute-start) | collective-permute-done | bytes 288 | tf_op jit(solution)/shard_map/ppermute | solution.py:238
  3.9 0.0 collective-permute-done.1
  3.9 0.8 %pack.1 = f32[40,128]{1,0:T(8,128)S(1)} custom-call(f32[32,128]{1,0:T(8,128)S(1)} %get-tuple-element.7.kept_ref, s32[1,64]{1,0:T(1,128)} %bitcast.13, s32[2,64]{1,0:T(2,128)} %bitcast.12, s32[1,64]{1,0:T(1,128)S(1)} %bitcast.11, s32[2,64]{1,0:T(2,128)S(1)} %bitcast.10), custom_call_target="tpu_custom_call" | custom-call | tf_op jit(solution)/shard_map/pack/pallas_call | solution.py:276
  4.7 0.0 collective-permute-done.2
  4.7 2.7 %collective-permute-start.3 = (f32[24,128]{1,0:T(8,128)S(1)}, f32[24,128]{1,0:T(8,128)S(1)}, u32[]{:S(2)}, u32[]{:S(2)}) collective-permute-start(f32[24,128]{1,0:T(8,128)S(1)} %slice_add_fusion.after_ref), channel_id=1, source_target_pairs={{0,3},{1,2},{2,1},{3,0},{4,7},{5,6},{6,5},{7,4},{8,11},{9,10},{10,... | collective-permute-start | bytes 36872 | tf_op jit(solution)/shard_map/ppermute | solution.py:238
  7.4 1.4 %collective-permute-done.3 = f32[24,128]{1,0:T(8,128)S(1)} collective-permute-done((f32[24,128]{1,0:T(8,128)S(1)}, f32[24,128]{1,0:T(8,128)S(1)}, u32[]{:S(2)}, u32[]{:S(2)}) %collective-permute-start.3) | collective-permute-done | bytes 12320 | tf_op jit(solution)/shard_map/ppermute | solution.py:238
  8.8 1.8 %collective-permute-start.4 = (f32[16,128]{1,0:T(8,128)S(1)}, f32[16,128]{1,0:T(8,128)S(1)}, u32[]{:S(2)}, u32[]{:S(2)}) collective-permute-start(f32[16,128]{1,0:T(8,128)S(1)} %slice_add_fusion.1), channel_id=1, source_target_pairs={{0,5},{1,4},{2,7},{3,6},{4,1},{5,0},{6,3},{7,2},{8,13},{9,12},{10,... | collective-permute-start | bytes 24584 | tf_op jit(solution)/shard_map/ppermute | solution.py:238
  10.6 1.2 %fetch.1.transfer_ref = bf16[1,2,256,1024]{3,2,1,0:T(8,128)(2,1)S(1)} custom-call(f32[24,128]{1,0:T(8,128)S(1)} %slice_add_fusion.after_ref, bf16[1,2,256,1024]{3,2,1,0:T(8,128)(2,1)} %transfer_hbm.1), custom_call_target="tpu_custom_call" | custom-call | tf_op jit(solution)/shard_map/fetch/pallas_call | solution.py:302
  11.9 0.1 collective-permute-done.4
  12.0 2.8 %collective-permute-start.5 = (f32[20,128]{1,0:T(8,128)S(1)}, f32[20,128]{1,0:T(8,128)S(1)}, u32[]{:S(2)}, u32[]{:S(2)}) collective-permute-start(f32[20,128]{1,0:T(8,128)S(1)} %pad_maximum_fusion), channel_id=1, source_target_pairs={{0,9},{1,8},{2,11},{3,10},{4,13},{5,12},{6,15},{7,14},{8,1},{9,0},... | collective-permute-start | bytes 30728 | tf_op jit(solution)/shard_map/ppermute | solution.py:238
  14.8 0.2 count.1.count_ref
  15.0 0.3 %turn.1.turned_ref = bf16[1,1024,512]{2,1,0:T(8,128)(2,1)S(1)} custom-call(f32[16,128]{1,0:T(8,128)S(1)} %pad_maximum_fusion.2.held_ref.after_ref, bf16[1,2,256,1024]{3,2,1,0:T(8,128)(2,1)S(1)} %fetch.1.transfer_ref), custom_call_target="tpu_custom_call" | custom-call | tf_op jit(solution)/shard_map/turn/pallas_call | solution.py:321
  15.3 0.9 %collective-permute-done.5.got_ref = f32[20,128]{1,0:T(8,128)S(1)} collective-permute-done((f32[20,128]{1,0:T(8,128)S(1)}, f32[20,128]{1,0:T(8,128)S(1)}, u32[]{:S(2)}, u32[]{:S(2)}) %collective-permute-start.5) | collective-permute-done | bytes 10272 | tf_op jit(solution)/shard_map/ppermute | solution.py:238
  16.2 1.2 %residual.1 = f32[1,2,1024]{2,1,0:T(2,128)} custom-call(f32[1,32,128]{2,1,0:T(8,128)S(1)} %count.1.count_ref, f32[4,128]{1,0:T(4,128)S(1)} %get-tuple-element.12.held_ref, f32[20,128]{1,0:T(8,128)S(1)} %collective-permute-done.5.got_ref, bf16[1,2,256,1024]{3,2,1,0:T(8,128)(2,1)S(1)} %fetch.1.transfer_ref, bf16[1,1024,512]{2,1,0:T(8,128)(2,1)S(1)} %turn.1.turned_ref), custom_call_target="tpu_custom_call" | custom-call | tf_op jit(solution)/shard_map/residual/pallas_call | solution.py:329
  (8 shorter events, 0.0 us)
Async XLA Ops:
  0.0 1.2 %copy-start = (f32[512,2,256]{2,1,0:T(2,128)S(1)}, f32[512,2,256]{2,1,0:T(2,128)}, u32[]{:S(2)}) copy-start(f32[512,2,256]{2,1,0:T(2,128)} %param.5) | copy-start | bytes 3145732
  1.5 0.7 %copy-start.1 = (s32[64,2]{0,1:T(2,128)S(1)}, s32[64,2]{0,1:T(2,128)}, u32[]{:S(2)}) copy-start(s32[64,2]{0,1:T(2,128)} %param.9) | copy-start | bytes 1540
  1.5 1.2 %copy-start.2 = (s32[64]{0:T(128)S(1)}, s32[64]{0:T(128)}, u32[]{:S(2)}) copy-start(s32[64]{0:T(128)} %param.8) | copy-start | bytes 772
  1.6 3.1 %collective-permute-start.2 = (f32[40,128]{1,0:T(8,128)S(1)}, f32[40,128]{1,0:T(8,128)S(1)}, u32[]{:S(2)}, u32[]{:S(2)}) collective-permute-start(f32[40,128]{1,0:T(8,128)S(1)} %get-tuple-element.8), channel_id=1, source_target_pairs={{0,1},{1,0},{2,3},{3,2},{4,5},{5,4},{6,7},{7,6},{8,9},{9,8},{10,11... | collective-permute-start | bytes 61448 | tf_op jit(solution)/shard_map/ppermute | solution.py:238
  2.2 1.7 %collective-permute-start.1 = (s32[64,2]{0,1:T(2,128)S(1)}, s32[64,2]{0,1:T(2,128)S(1)}, u32[]{:S(2)}, u32[]{:S(2)}) collective-permute-start(s32[64,2]{0,1:T(2,128)S(1)} %copy-done.1), channel_id=1, source_target_pairs={{0,1},{1,0},{2,3},{3,2},{4,5},{5,4},{6,7},{7,6},{8,9},{9,8},{10,11... | collective-permute-start | bytes 1544 | tf_op jit(solution)/shard_map/ppermute | solution.py:238
  2.7 1.2 %collective-permute-start = (s32[64]{0:T(128)S(1)}, s32[64]{0:T(128)S(1)}, u32[]{:S(2)}, u32[]{:S(2)}) collective-permute-start(s32[64]{0:T(128)S(1)} %copy-done.2), channel_id=1, source_target_pairs={{0,1},{1,0},{2,3},{3,2},{4,5},{5,4},{6,7},{7,6},{8,9},{9,8},{10,11... | collective-permute-start | bytes 776 | tf_op jit(solution)/shard_map/ppermute | solution.py:238
  4.7 4.1 %collective-permute-start.3 = (f32[24,128]{1,0:T(8,128)S(1)}, f32[24,128]{1,0:T(8,128)S(1)}, u32[]{:S(2)}, u32[]{:S(2)}) collective-permute-start(f32[24,128]{1,0:T(8,128)S(1)} %slice_add_fusion.after_ref), channel_id=1, source_target_pairs={{0,3},{1,2},{2,1},{3,0},{4,7},{5,6},{6,5},{7,4},{8,11},{9,10},{10,... | collective-permute-start | bytes 36872 | tf_op jit(solution)/shard_map/ppermute | solution.py:238
  8.8 3.2 %collective-permute-start.4 = (f32[16,128]{1,0:T(8,128)S(1)}, f32[16,128]{1,0:T(8,128)S(1)}, u32[]{:S(2)}, u32[]{:S(2)}) collective-permute-start(f32[16,128]{1,0:T(8,128)S(1)} %slice_add_fusion.1), channel_id=1, source_target_pairs={{0,5},{1,4},{2,7},{3,6},{4,1},{5,0},{6,3},{7,2},{8,13},{9,12},{10,... | collective-permute-start | bytes 24584 | tf_op jit(solution)/shard_map/ppermute | solution.py:238
  12.0 4.2 %collective-permute-start.5 = (f32[20,128]{1,0:T(8,128)S(1)}, f32[20,128]{1,0:T(8,128)S(1)}, u32[]{:S(2)}, u32[]{:S(2)}) collective-permute-start(f32[20,128]{1,0:T(8,128)S(1)} %pad_maximum_fusion), channel_id=1, source_target_pairs={{0,9},{1,8},{2,11},{3,10},{4,13},{5,12},{6,15},{7,14},{8,1},{9,0},... | collective-permute-start | bytes 30728 | tf_op jit(solution)/shard_map/ppermute | solution.py:238
